TPU v7x, 512 devices: a whole 4x4x16 slice. The times are simulated.
512 devices in a mesh: comp: 4 (over y_hi, core), tile: 128 (over z, y_lo, x).
Axes of the slice: x: 4, y: 4 (y_hi: 2, y_lo: 2; y = y_hi * 2 + y_lo), z: 16, core: 2. Of those that a mesh axis runs over, the one named last changes fastest.
Arguments:
- column_state: float32 [4, 128, 4, 16, 2048], P('comp', 'tile'), may hold values from -6 to 6
- mixing: float32 [2, 4, 16], replicated, may hold values from 0.02 to 0.24
- vertical: float32 [2, 16, 16], replicated, may hold values from -1.5 to 1.5
- flux_coef: float32 [2, 4], replicated, may hold values from 0.5 to 1.5
- atm_block: int32 [4, 128, 16], P('comp', 'tile'), may hold values from 0 to 15
- ocean_block: int32 [4, 128, 16], P('comp', 'tile'), may hold values from 0 to 15
- tile_offset: int32 [4, 128, 16], P('comp', 'tile'), may hold values from 0 to 6
- remap_weights: bfloat16 [4, 128, 16, 128, 128], P('comp', 'tile'), may hold values from 0 to 0.119628906
- ocean_mask: int32 [128, 2048], P('tile'), may hold values 0 or 1
Outputs:
- new_state: float32 [4, 128, 4, 16, 2048], P('comp', 'tile')
Inputs may be any that keep to these rules, and one draw needn't show every extreme that they name: `atm_block`: entries at comp index 3 are not read.
All inputs are finite; a program needn't handle non-finite values. No bound on the sum of `ocean_mask` on one device may be relied on, other than what follows from the above.
Results may differ from a plain program's by a relative error of at most 0.0003.
Values sent between devices are 32-bit elements; how exact they have to be, the bound alone decides.
A program may use at most 64 MiB of HBM per device.

v0:
```python
import jax
import jax.numpy as jnp
from jax import lax
from jax.sharding import PartitionSpec as P

REACH = 3
SUB = 2


def extended(cells, sides, width):
    for axis, dim in sides:
        count = lax.axis_size(axis)
        head = lax.slice_in_dim(cells, 0, width, axis=dim)
        tail = lax.slice_in_dim(cells, cells.shape[dim] - width, cells.shape[dim], axis=dim)
        cells = jnp.concatenate(
            [
                lax.ppermute(tail, axis, [(i, (i + 1) % count) for i in range(count)]),
                cells,
                lax.ppermute(head, axis, [((i + 1) % count, i) for i in range(count)]),
            ],
            axis=dim,
        )
    return cells


def passed_along(value, axis, steps):
    count = lax.axis_size(axis)
    pairs = [(source, (source + steps) % count) for source in range(count)]
    return lax.ppermute(value, axis, pairs)


def gathered_total(array, axis):
    return lax.all_gather(array, axis).sum(0)


def local(
    column_state,
    mixing,
    vertical,
    flux_coef,
    atm_block,
    ocean_block,
    tile_offset,
    remap_weights,
    ocean_mask,
):
    fields = column_state[0, 0]
    cells = fields.shape[2]
    across = remap_weights.shape[3]
    ocean_cells = remap_weights.shape[4]
    oblocks = cells // ocean_cells
    spread = 2 * REACH + 1
    comp_index = lax.axis_index("comp")
    comp_count = lax.axis_size("comp")
    is_atmos = comp_index < comp_count - 1
    group = jnp.where(is_atmos, 0, 1).astype(jnp.int32)
    rates = lax.dynamic_index_in_dim(mixing, group, 0, keepdims=False)[:, :, None]
    operator = lax.dynamic_index_in_dim(vertical, group, 0, keepdims=False)
    for sweep in range(SUB):
        padded = extended(fields, (("tile", 2),), 1)
        fields = fields + rates * (padded[:, :, :-2] + padded[:, :, 2:] - 2.0 * fields)
    mixed = fields + jnp.einsum("lm,kmz->klz", operator, fields, precision=lax.Precision.HIGHEST)
    surface = jnp.tanh(flux_coef[0][:, None] * mixed[:, -1] + flux_coef[1][:, None] * mixed[:, -2])
    rounded = surface.astype(jnp.bfloat16)
    blocks = rounded.reshape(rounded.shape[0], cells // across, across)
    chosen = blocks[:, atm_block[0, 0], :]
    contrib = jnp.einsum(
        "knb,nbj->nkj", chosen, remap_weights[0, 0], preferred_element_type=jnp.float32
    )
    by_offset = (tile_offset[0, 0][:, None] == jnp.arange(spread, dtype=jnp.int32)[None, :]).astype(
        jnp.float32
    )
    by_block = (ocean_block[0, 0][:, None] == jnp.arange(oblocks, dtype=jnp.int32)[None, :]).astype(
        jnp.float32
    )
    buffers = jnp.einsum(
        "nd,no,nkj->dkoj", by_offset, by_block, contrib, precision=lax.Precision.HIGHEST
    )
    buffers = buffers.reshape(spread, rounded.shape[0], cells)
    buffers = jnp.where(is_atmos, buffers, 0.0)
    received = buffers[REACH]
    for offset in range(-REACH, REACH + 1):
        if offset != 0:
            received = received + passed_along(buffers[REACH + offset], "tile", offset)
    received = gathered_total(received, "comp")
    land = ocean_mask[0].astype(jnp.float32)
    atmosphere = mixed.at[:, -1].add(-0.5 * surface)
    ocean = mixed.at[:, 0].add(land[None, :] * received)
    result = jnp.where(is_atmos, atmosphere, ocean)
    return result[None, None]


def solution(mesh):
    placed = (
        P("comp", "tile", None, None, None),
        P(),
        P(),
        P(),
        P("comp", "tile", None),
        P("comp", "tile", None),
        P("comp", "tile", None),
        P("comp", "tile", None, None, None),
        P("tile", None),
    )
    return jax.shard_map(
        local,
        mesh=mesh,
        in_specs=placed,
        out_specs=P("comp", "tile", None, None, None),
        check_vma=False,
    )
```

profile of v0, /device:TPU:5, one launch (start us, length us, event | category | flops | bytes accessed | tf_op | source)
XLA Modules:
  0.0 76.3 jit_solution(2108912572407829848)
XLA Ops:
  0.0 0.0 copy-start
  0.0 1.4 %copy.49 = f32[1,1,4,16,2048]{4,2,3,1,0:T(4,128)S(1)} copy(f32[1,1,4,16,2048]{4,3,2,1,0:T(8,128)} %param.13) | data formatting | bytes 1048576 | tf_op args[0]
  1.4 0.1 fusion.37
  1.5 2.8 %collective-permute-start = (f32[4,16,1]{2,0,1:T(4,128)S(1)}, f32[4,16,1]{2,0,1:T(4,128)S(1)}, u32[]{:S(2)}, u32[]{:S(2)}) collective-permute-start(f32[4,16,1]{2,0,1:T(4,128)S(1)} %get-tuple-element.35), channel_id=1, source_target_pairs={{0,1},{1,2},{2,3},{3,4},{4,5},{5,6},{6,7},{7,8},{8,9},{9,10},{10,1... | collective-permute-start | bytes 776 | tf_op jit(solution)/shard_map/ppermute | solution.py:17
  4.4 2.5 %collective-permute-start.1 = (f32[4,16,1]{2,0,1:T(4,128)S(1)}, f32[4,16,1]{2,0,1:T(4,128)S(1)}, u32[]{:S(2)}, u32[]{:S(2)}) collective-permute-start(f32[4,16,1]{2,0,1:T(4,128)S(1)} %get-tuple-element.36), channel_id=1, source_target_pairs={{1,0},{2,1},{3,2},{4,3},{5,4},{6,5},{7,6},{8,7},{9,8},{10,9},{11,1... | collective-permute-start | bytes 776 | tf_op jit(solution)/shard_map/ppermute | solution.py:19
  6.8 0.0 copy-start.4
  6.8 0.7 copy-done.4
  7.5 0.6 copy-done.7
  8.2 0.7 copy-done.5
  8.8 0.7 copy-done.6
  9.5 0.7 copy-done.3
  10.2 0.1 copy.16
  10.3 0.0 collective-permute-done
  10.3 0.0 collective-permute-done.1
  10.3 0.6 fusion.8
  10.9 0.1 fusion.36
  11.0 4.0 %collective-permute-start.2 = (f32[4,16,1]{2,0,1:T(4,128)S(1)}, f32[4,16,1]{2,0,1:T(4,128)S(1)}, u32[]{:S(2)}, u32[]{:S(2)}) collective-permute-start(f32[4,16,1]{2,0,1:T(4,128)S(1)} %get-tuple-element.33), channel_id=1, source_target_pairs={{0,1},{1,2},{2,3},{3,4},{4,5},{5,6},{6,7},{7,8},{8,9},{9,10},{10,1... | collective-permute-start | bytes 776 | tf_op jit(solution)/shard_map/ppermute | solution.py:17
  15.0 1.9 %collective-permute-start.3 = (f32[4,16,1]{2,0,1:T(4,128)S(1)}, f32[4,16,1]{2,0,1:T(4,128)S(1)}, u32[]{:S(2)}, u32[]{:S(2)}) collective-permute-start(f32[4,16,1]{2,0,1:T(4,128)S(1)} %get-tuple-element.34), channel_id=1, source_target_pairs={{1,0},{2,1},{3,2},{4,3},{5,4},{6,5},{7,6},{8,7},{9,8},{10,9},{11,1... | collective-permute-start | bytes 776 | tf_op jit(solution)/shard_map/ppermute | solution.py:19
  16.9 0.0 copy-start.2
  16.9 0.0 collective-permute-done.2
  16.9 3.4 %collective-permute-done.3 = f32[4,16,1]{2,0,1:T(4,128)S(1)} collective-permute-done((f32[4,16,1]{2,0,1:T(4,128)S(1)}, f32[4,16,1]{2,0,1:T(4,128)S(1)}, u32[]{:S(2)}, u32[]{:S(2)}) %collective-permute-start.3) | collective-permute-done | bytes 288 | tf_op jit(solution)/shard_map/ppermute | solution.py:19
  20.4 0.6 fusion.4
  21.0 0.0 copy-done.2
  21.0 0.9 %fusion.11 = f32[4,2048,16]{1,2,0:T(8,128)S(1)} fusion(f32[4,16,2048]{2,0,1:T(4,128)S(1)} %fusion.4, f32[2,16,16]{2,1,0:T(8,128)S(1)} %copy-done.2, s32[]{:T(128)S(6)} %select_n.39), kind=kOutput, calls=%fused_computation.18 | convolution fusion | flops 25165824 | bytes 1056772 | tf_op jit(solution)/shard_map/lm,kmz->klz/dot_general | solution.py:62
  21.9 0.7 bitcast_add_fusion
  22.6 0.1 fusion.23
  22.7 0.6 gather_fusion
  23.3 0.0 copy-done
  23.3 0.2 fusion.9
  23.5 0.3 fusion
  23.9 18.4 %collective-permute-start.4 = (f32[4,2048]{1,0:T(4,128)S(1)}, f32[4,2048]{1,0:T(4,128)S(1)}, u32[]{:S(2)}, u32[]{:S(2)}) collective-permute-start(f32[4,2048]{1,0:T(4,128)S(1)} %bitcast.123), channel_id=1, source_target_pairs={{0,125},{1,126},{2,127},{3,0},{4,1},{5,2},{6,3},{7,4},{8,5},{9,6},... | collective-permute-start | bytes 98312 | tf_op jit(solution)/shard_map/ppermute | solution.py:29
  42.4 1.9 %collective-permute-start.5 = (f32[4,2048]{1,0:T(4,128)S(1)}, f32[4,2048]{1,0:T(4,128)S(1)}, u32[]{:S(2)}, u32[]{:S(2)}) collective-permute-start(f32[4,2048]{1,0:T(4,128)S(1)} %bitcast.121), channel_id=1, source_target_pairs={{0,126},{1,127},{2,0},{3,1},{4,2},{5,3},{6,4},{7,5},{8,6},{9,7},{1... | collective-permute-start | bytes 98312 | tf_op jit(solution)/shard_map/ppermute | solution.py:29
  44.3 3.1 %collective-permute-start.6 = (f32[4,2048]{1,0:T(4,128)S(1)}, f32[4,2048]{1,0:T(4,128)S(1)}, u32[]{:S(2)}, u32[]{:S(2)}) collective-permute-start(f32[4,2048]{1,0:T(4,128)S(1)} %bitcast.122), channel_id=1, source_target_pairs={{0,127},{1,0},{2,1},{3,2},{4,3},{5,4},{6,5},{7,6},{8,7},{9,8},{10,... | collective-permute-start | bytes 98312 | tf_op jit(solution)/shard_map/ppermute | solution.py:29
  47.4 2.2 %collective-permute-start.7 = (f32[4,2048]{1,0:T(4,128)S(1)}, f32[4,2048]{1,0:T(4,128)S(1)}, u32[]{:S(2)}, u32[]{:S(2)}) collective-permute-start(f32[4,2048]{1,0:T(4,128)S(1)} %bitcast.124), channel_id=1, source_target_pairs={{0,1},{1,2},{2,3},{3,4},{4,5},{5,6},{6,7},{7,8},{8,9},{9,10},{10,1... | collective-permute-start | bytes 98312 | tf_op jit(solution)/shard_map/ppermute | solution.py:29
  49.7 5.8 %collective-permute-start.8 = (f32[4,2048]{1,0:T(4,128)S(1)}, f32[4,2048]{1,0:T(4,128)S(1)}, u32[]{:S(2)}, u32[]{:S(2)}) collective-permute-start(f32[4,2048]{1,0:T(4,128)S(1)} %bitcast.125), channel_id=1, source_target_pairs={{0,2},{1,3},{2,4},{3,5},{4,6},{5,7},{6,8},{7,9},{8,10},{9,11},{10,... | collective-permute-start | bytes 98312 | tf_op jit(solution)/shard_map/ppermute | solution.py:29
  55.4 0.0 copy-start.1
  55.5 0.0 collective-permute-done.4
  55.5 1.9 %collective-permute-start.9 = (f32[4,2048]{1,0:T(4,128)S(1)}, f32[4,2048]{1,0:T(4,128)S(1)}, u32[]{:S(2)}, u32[]{:S(2)}) collective-permute-start(f32[4,2048]{1,0:T(4,128)S(1)} %bitcast.126), channel_id=1, source_target_pairs={{0,3},{1,4},{2,5},{3,6},{4,7},{5,8},{6,9},{7,10},{8,11},{9,12},{10... | collective-permute-start | bytes 98312 | tf_op jit(solution)/shard_map/ppermute | solution.py:29
  57.4 0.0 copy-done.1
  57.5 0.0 collective-permute-done.5
  57.5 0.0 collective-permute-done.6
  57.5 0.0 collective-permute-done.7
  57.5 0.0 collective-permute-done.8
  57.5 5.6 %collective-permute-done.9 = f32[4,2048]{1,0:T(4,128)S(1)} collective-permute-done((f32[4,2048]{1,0:T(4,128)S(1)}, f32[4,2048]{1,0:T(4,128)S(1)}, u32[]{:S(2)}, u32[]{:S(2)}) %collective-permute-start.9) | collective-permute-done | bytes 32800 | tf_op jit(solution)/shard_map/ppermute | solution.py:29
  63.2 11.7 %all-gather.1 = f32[4,4,2048]{2,1,0:T(4,128)S(1)} all-gather(f32[1,4,2048]{2,1,0:T(4,128)S(1)} %fusion.20), channel_id=2, replica_groups=mesh['comp'=4,'tile'=128] {'comp'}, dimensions={0}, use_global_device_ids=true | all-gather | bytes 163840 | tf_op jit(solution)/shard_map/all_gather | solution.py:33
  74.9 0.1 add_dynamic-update-slice_fusion
  75.0 0.1 select_bitcast_fusion
  75.2 1.1 %copy.21 = f32[1,1,4,16,2048]{4,3,2,1,0:T(8,128)} copy(f32[1,1,4,16,2048]{4,2,3,1,0:T(4,128)S(1)} %select_bitcast_fusion) | data formatting | bytes 1048576 | tf_op jit(solution)/shard_map/broadcast_in_dim | solution.py:90
  (24 shorter events, 0.3 us)
Async XLA Ops:
  0.0 23.3 %copy-start = (bf16[1,1,16,128,128]{4,3,2,1,0:T(8,128)(2,1)S(1)}, bf16[1,1,16,128,128]{4,3,2,1,0:T(8,128)(2,1)}, u32[]{:S(2)}) copy-start(bf16[1,1,16,128,128]{4,3,2,1,0:T(8,128)(2,1)} %param.20) | copy-start | bytes 1572868
  1.5 8.7 %collective-permute-start = (f32[4,16,1]{2,0,1:T(4,128)S(1)}, f32[4,16,1]{2,0,1:T(4,128)S(1)}, u32[]{:S(2)}, u32[]{:S(2)}) collective-permute-start(f32[4,16,1]{2,0,1:T(4,128)S(1)} %get-tuple-element.35), channel_id=1, source_target_pairs={{0,1},{1,2},{2,3},{3,4},{4,5},{5,6},{6,7},{7,8},{8,9},{9,10},{10,1... | collective-permute-start | bytes 776 | tf_op jit(solution)/shard_map/ppermute | solution.py:17
  4.4 5.9 %collective-permute-start.1 = (f32[4,16,1]{2,0,1:T(4,128)S(1)}, f32[4,16,1]{2,0,1:T(4,128)S(1)}, u32[]{:S(2)}, u32[]{:S(2)}) collective-permute-start(f32[4,16,1]{2,0,1:T(4,128)S(1)} %get-tuple-element.36), channel_id=1, source_target_pairs={{1,0},{2,1},{3,2},{4,3},{5,4},{6,5},{7,6},{8,7},{9,8},{10,9},{11,1... | collective-permute-start | bytes 776 | tf_op jit(solution)/shard_map/ppermute | solution.py:19
  6.8 0.7 copy-start.4
  7.5 0.7 copy-start.7
  8.2 0.7 copy-start.5
  8.8 0.7 copy-start.6
  9.5 0.7 copy-start.3
  11.0 5.9 %collective-permute-start.2 = (f32[4,16,1]{2,0,1:T(4,128)S(1)}, f32[4,16,1]{2,0,1:T(4,128)S(1)}, u32[]{:S(2)}, u32[]{:S(2)}) collective-permute-start(f32[4,16,1]{2,0,1:T(4,128)S(1)} %get-tuple-element.33), channel_id=1, source_target_pairs={{0,1},{1,2},{2,3},{3,4},{4,5},{5,6},{6,7},{7,8},{8,9},{9,10},{10,1... | collective-permute-start | bytes 776 | tf_op jit(solution)/shard_map/ppermute | solution.py:17
  15.0 5.4 %collective-permute-start.3 = (f32[4,16,1]{2,0,1:T(4,128)S(1)}, f32[4,16,1]{2,0,1:T(4,128)S(1)}, u32[]{:S(2)}, u32[]{:S(2)}) collective-permute-start(f32[4,16,1]{2,0,1:T(4,128)S(1)} %get-tuple-element.34), channel_id=1, source_target_pairs={{1,0},{2,1},{3,2},{4,3},{5,4},{6,5},{7,6},{8,7},{9,8},{10,9},{11,1... | collective-permute-start | bytes 776 | tf_op jit(solution)/shard_map/ppermute | solution.py:19
  16.9 4.1 %copy-start.2 = (f32[2,16,16]{2,1,0:T(8,128)S(1)}, f32[2,16,16]{2,1,0:T(8,128)}, u32[]{:S(2)}) copy-start(f32[2,16,16]{2,1,0:T(8,128)} %param.15) | copy-start | bytes 6148
  23.9 31.6 %collective-permute-start.4 = (f32[4,2048]{1,0:T(4,128)S(1)}, f32[4,2048]{1,0:T(4,128)S(1)}, u32[]{:S(2)}, u32[]{:S(2)}) collective-permute-start(f32[4,2048]{1,0:T(4,128)S(1)} %bitcast.123), channel_id=1, source_target_pairs={{0,125},{1,126},{2,127},{3,0},{4,1},{5,2},{6,3},{7,4},{8,5},{9,6},... | collective-permute-start | bytes 98312 | tf_op jit(solution)/shard_map/ppermute | solution.py:29
  42.4 15.1 %collective-permute-start.5 = (f32[4,2048]{1,0:T(4,128)S(1)}, f32[4,2048]{1,0:T(4,128)S(1)}, u32[]{:S(2)}, u32[]{:S(2)}) collective-permute-start(f32[4,2048]{1,0:T(4,128)S(1)} %bitcast.121), channel_id=1, source_target_pairs={{0,126},{1,127},{2,0},{3,1},{4,2},{5,3},{6,4},{7,5},{8,6},{9,7},{1... | collective-permute-start | bytes 98312 | tf_op jit(solution)/shard_map/ppermute | solution.py:29
  44.3 13.2 %collective-permute-start.6 = (f32[4,2048]{1,0:T(4,128)S(1)}, f32[4,2048]{1,0:T(4,128)S(1)}, u32[]{:S(2)}, u32[]{:S(2)}) collective-permute-start(f32[4,2048]{1,0:T(4,128)S(1)} %bitcast.122), channel_id=1, source_target_pairs={{0,127},{1,0},{2,1},{3,2},{4,3},{5,4},{6,5},{7,6},{8,7},{9,8},{10,... | collective-permute-start | bytes 98312 | tf_op jit(solution)/shard_map/ppermute | solution.py:29
  47.4 10.1 %collective-permute-start.7 = (f32[4,2048]{1,0:T(4,128)S(1)}, f32[4,2048]{1,0:T(4,128)S(1)}, u32[]{:S(2)}, u32[]{:S(2)}) collective-permute-start(f32[4,2048]{1,0:T(4,128)S(1)} %bitcast.124), channel_id=1, source_target_pairs={{0,1},{1,2},{2,3},{3,4},{4,5},{5,6},{6,7},{7,8},{8,9},{9,10},{10,1... | collective-permute-start | bytes 98312 | tf_op jit(solution)/shard_map/ppermute | solution.py:29
  49.7 7.9 %collective-permute-start.8 = (f32[4,2048]{1,0:T(4,128)S(1)}, f32[4,2048]{1,0:T(4,128)S(1)}, u32[]{:S(2)}, u32[]{:S(2)}) collective-permute-start(f32[4,2048]{1,0:T(4,128)S(1)} %bitcast.125), channel_id=1, source_target_pairs={{0,2},{1,3},{2,4},{3,5},{4,6},{5,7},{6,8},{7,9},{8,10},{9,11},{10,... | collective-permute-start | bytes 98312 | tf_op jit(solution)/shard_map/ppermute | solution.py:29
  55.4 2.0 %copy-start.1 = (s32[1,2048]{1,0:T(1,128)S(1)}, s32[1,2048]{1,0:T(1,128)}, u32[]{:S(2)}) copy-start(s32[1,2048]{1,0:T(1,128)} %param.21) | copy-start | bytes 24580
  55.5 7.7 %collective-permute-start.9 = (f32[4,2048]{1,0:T(4,128)S(1)}, f32[4,2048]{1,0:T(4,128)S(1)}, u32[]{:S(2)}, u32[]{:S(2)}) collective-permute-start(f32[4,2048]{1,0:T(4,128)S(1)} %bitcast.126), channel_id=1, source_target_pairs={{0,3},{1,4},{2,5},{3,6},{4,7},{5,8},{6,9},{7,10},{8,11},{9,12},{10... | collective-permute-start | bytes 98312 | tf_op jit(solution)/shard_map/ppermute | solution.py:29
where the time goes:
time: 76.9 us; the launch traced here: 76.3 us
  starting transfers between devices  44.5 us (58%)
  blocking collectives  11.7 us (15%)
  waiting for transfers between devices  9.05 us (12%)
  local copies, waits for them, and re-layouts  6.89 us (9%)
  other arithmetic  2.38 us (3%)
  matrix products  1.45 us (2%)
    ppermute x6, starting transfers between devices, passed_along(): return lax.ppermute(value, axis, pairs)  33.3 us
    all_gather x1, blocking collectives, gathered_total(): return lax.all_gather(array, axis).sum(0)  11.7 us
    ppermute x2, starting transfers between devices, extended(): lax.ppermute(tail, axis, [(i, (i + 1) % count) for i in range(count)])  6.79 us
    ppermute x6, waiting for transfers between devices, passed_along(): return lax.ppermute(value, axis, pairs)  5.63 us
    unnamed x26, local copies, waits for them, and re-layouts  4.93 us
    ppermute x2, starting transfers between devices, extended(): lax.ppermute(head, axis, [((i + 1) % count, i) for i in range(count)])  4.38 us
    ppermute x2, waiting for transfers between devices, extended(): lax.ppermute(head, axis, [((i + 1) % count, i) for i in range(count)])  3.41 us
  transfers between devices with their start and end apart: 10, of which 2 were waited for; matrix products, arithmetic and copies ran while one was open for 0% of the time, Pallas kernels for 0%

commit v1 on v0

v1 whole, which is shorter than its diff:
```python
import functools

import jax
import jax.numpy as jnp
from jax import lax
from jax.experimental import pallas as pl
from jax.experimental.pallas import tpu as pltpu
from jax.sharding import PartitionSpec as P

REACH = 3
SPREAD = 2 * REACH + 1
MESH = pl.DeviceIdType.MESH
F32 = jnp.float32
BF16 = jnp.bfloat16
LANES = 128
SURF = 16


def iota(shape, dim):
    return lax.broadcasted_iota(jnp.int32, shape, dim)


def column(row, count):
    wide = jnp.broadcast_to(row, (count, row.shape[1]))
    keep = iota(wide.shape, 0) == iota(wide.shape, 1)
    return jnp.sum(jnp.where(keep, wide, 0.0), axis=1, keepdims=True)


def split2(x):
    hi = x.astype(BF16)
    lo = (x - hi.astype(F32)).astype(BF16)
    return hi, lo


def kernel(
    dims,
    state,
    mixing,
    vertical,
    flux,
    ablk,
    oblk,
    toff,
    weights,
    mask,
    out,
    f,
    mix_v,
    ver_v,
    flux_v,
    ablk_s,
    oblk_v,
    toff_v,
    w_v,
    mask_v,
    coef,
    opmat,
    pack,
    halo,
    surf,
    contrib,
    dense,
    recv,
    rx,
    load_sem,
    halo_send,
    halo_recv,
    dense_send,
    dense_recv,
):
    fields, lev, cells, comps, tiles, nb = dims
    rows = fields * lev
    ntile = cells // LANES
    oblocks = cells // LANES
    c = lax.axis_index("comp")
    t = lax.axis_index("tile")
    ocean_row = comps - 1
    is_atmos = c < ocean_row
    is_ocean = c == ocean_row
    group = jnp.where(is_atmos, 0, 1)
    left = lax.rem(t + tiles - 1, tiles)
    right = lax.rem(t + 1, tiles)

    loads = [
        pltpu.make_async_copy(state.at[:, pl.ds(0, LANES)], f.at[:, pl.ds(LANES, LANES)], load_sem.at[0]),
        pltpu.make_async_copy(
            state.at[:, pl.ds(cells - LANES, LANES)], f.at[:, pl.ds(cells, LANES)], load_sem.at[1]
        ),
        pltpu.make_async_copy(
            state.at[:, pl.ds(LANES, cells - 2 * LANES)],
            f.at[:, pl.ds(2 * LANES, cells - 2 * LANES)],
            load_sem.at[2],
        ),
        pltpu.make_async_copy(mixing, mix_v, load_sem.at[3]),
        pltpu.make_async_copy(vertical, ver_v, load_sem.at[4]),
        pltpu.make_async_copy(flux, flux_v, load_sem.at[5]),
        pltpu.make_async_copy(ablk, ablk_s, load_sem.at[6]),
        pltpu.make_async_copy(oblk, oblk_v, load_sem.at[7]),
        pltpu.make_async_copy(toff, toff_v, load_sem.at[8]),
        pltpu.make_async_copy(weights, w_v, load_sem.at[9]),
        pltpu.make_async_copy(mask, mask_v, load_sem.at[10]),
    ]
    barrier = pltpu.get_barrier_semaphore()
    for who in (left, right):
        pl.semaphore_signal(barrier, inc=1, device_id=(c, who), device_id_type=MESH)
    for load in loads:
        load.start()

    @pl.when(is_ocean)
    def _():
        for src in range(comps - 1):
            for d in range(-REACH, REACH + 1):
                who = lax.rem(t - d + tiles, tiles)
                pl.semaphore_signal(barrier, inc=1, device_id=(src, who), device_id_type=MESH)

    loads[0].wait()
    loads[1].wait()
    lane = iota((8, LANES), 1)
    groups = rows // 8
    first = jnp.zeros((8, LANES), F32)
    last = jnp.zeros((8, LANES), F32)
    for i in range(groups):
        here = lane // 2 == i
        a = f[8 * i : 8 * i + 8, LANES : 2 * LANES]
        b = f[8 * i : 8 * i + 8, cells : cells + LANES]
        first = jnp.where(here, pltpu.roll(a, 2 * i, 1) if i else a, first)
        last = jnp.where(here, pltpu.roll(b, 2 * i + 2, 1), last)
    pack[0] = first
    pack[1] = last

    loads[3].wait()
    loads[4].wait()
    loads[5].wait()
    mix_g = mix_v[group]
    rates = jnp.concatenate([column(mix_g[k : k + 1, :], lev) for k in range(fields)], axis=0)
    keep = 1.0 - 2.0 * rates
    coef[0] = jnp.broadcast_to(keep * keep + 2.0 * rates * rates, (rows, LANES))
    coef[1] = jnp.broadcast_to(2.0 * rates * keep, (rows, LANES))
    coef[2] = jnp.broadcast_to(rates * rates, (rows, LANES))
    ver_g = ver_v[group]
    spread_l = (lax.rem(iota((rows, lev), 0), lev) == iota((rows, lev), 1)).astype(F32)
    spread_r = (lax.rem(iota((lev, rows), 1), lev) == iota((lev, rows), 0)).astype(F32)
    hp = lax.Precision.HIGHEST
    tall = jnp.dot(spread_l, ver_g, precision=hp, preferred_element_type=F32)
    square = jnp.dot(tall, spread_r, precision=hp, preferred_element_type=F32)
    square = jnp.where(iota((rows, rows), 0) // lev == iota((rows, rows), 1) // lev, square, 0.0)
    fa = jnp.concatenate([column(flux_v[0:1, :], fields), jnp.zeros((SURF - fields, 1), F32)], axis=0)
    fb = jnp.concatenate([column(flux_v[1:2, :], fields), jnp.zeros((SURF - fields, 1), F32)], axis=0)
    who_row, who_col = iota((SURF, rows), 0), iota((SURF, rows), 1)
    pick = jnp.where(who_col == who_row * lev + lev - 1, fa, 0.0) + jnp.where(
        who_col == who_row * lev + lev - 2, fb, 0.0
    )
    linear = pick + jnp.dot(pick, square, precision=hp, preferred_element_type=F32)
    high = rows + SURF
    sq_hi, sq_lo = split2(jnp.concatenate([square, linear], axis=0))
    opmat[0:high] = sq_hi
    opmat[high : 2 * high] = sq_lo
    half = jnp.where(is_atmos, 0.5, 0.0)

    pl.semaphore_wait(barrier, jnp.where(is_atmos, 2 + SPREAD, 2))
    to_right = pltpu.make_async_remote_copy(
        src_ref=pack.at[1],
        dst_ref=halo.at[0],
        send_sem=halo_send.at[0],
        recv_sem=halo_recv.at[0],
        device_id=(c, right),
        device_id_type=MESH,
    )
    to_left = pltpu.make_async_remote_copy(
        src_ref=pack.at[0],
        dst_ref=halo.at[1],
        send_sem=halo_send.at[1],
        recv_sem=halo_recv.at[1],
        device_id=(c, left),
        device_id_type=MESH,
    )
    to_right.start()
    to_left.start()

    def stencil(x, i):
        n = x.shape[1]
        s = slice(8 * i, 8 * i + 8)
        wide = lambda v: jnp.concatenate([v] * (n // LANES), axis=1)
        near = pltpu.roll(x, 1, 1) + pltpu.roll(x, n - 1, 1)
        far = pltpu.roll(x, 2, 1) + pltpu.roll(x, n - 2, 1)
        return wide(coef[0, s]) * x + wide(coef[1, s]) * near + wide(coef[2, s]) * far

    def mix(x, spots):
        hi, lo = split2(x)
        p = jnp.dot(opmat[...], hi, preferred_element_type=F32)
        q = jnp.dot(opmat[0:high], lo, preferred_element_type=F32)
        added = p[0:high] + (p[high : 2 * high] + q)
        mixed = x + added[0:rows]
        flux_now = jnp.tanh(added[rows : rows + 8])
        for i, b in enumerate(spots):
            cols = slice(b * LANES, (b + 1) * LANES)
            part = slice(i * LANES, (i + 1) * LANES)
            s = flux_now[:, part]
            surf[b] = s
            for k in range(fields):
                base = k * lev
                out[base : base + lev - 8, cols] = mixed[base : base + lev - 8, part]
                moved = pltpu.roll(s, 7 - k, 0)
                low = iota((8, LANES), 0) == 7
                out[base + lev - 8 : base + lev, cols] = mixed[base + lev - 8 : base + lev, part] - jnp.where(
                    low, half * moved, 0.0
                )

    loads[2].wait()
    for i in range(groups):
        x = f[8 * i : 8 * i + 8, LANES : LANES + cells]
        y = stencil(x, i)
        out[8 * i : 8 * i + 8, LANES : cells - LANES] = y[:, LANES : cells - LANES]
    for j in range(LANES, cells - LANES, 2 * LANES):
        mix(out[:, j : j + 2 * LANES], (j // LANES, j // LANES + 1))

    to_right.wait()
    to_left.wait()
    hl = halo[0]
    hr = halo[1]
    for i in range(groups):
        s = slice(8 * i, 8 * i + 8)
        f[s, 0:LANES] = pltpu.roll(hl, LANES - 2 * i - 2, 1)
        f[s, LANES + cells : 2 * LANES + cells] = pltpu.roll(hr, LANES - 2 * i, 1) if i else hr
    lefts, rights = [], []
    for i in range(groups):
        s = slice(8 * i, 8 * i + 8)
        lefts.append(stencil(f[s, 0 : 3 * LANES], i)[:, LANES : 2 * LANES])
        rights.append(stencil(f[s, cells - LANES : cells + 2 * LANES], i)[:, LANES : 2 * LANES])
    edge = jnp.concatenate([jnp.concatenate(lefts, axis=0), jnp.concatenate(rights, axis=0)], axis=1)
    mix(edge, (0, ntile - 1))

    loads[6].wait()
    loads[7].wait()
    loads[8].wait()
    loads[9].wait()
    loads[10].wait()

    @pl.when(is_atmos)
    def _():
        for n in range(nb):
            picked = surf[ablk_s[n]].astype(BF16)
            part = jnp.dot(picked, w_v[n], preferred_element_type=F32)
            contrib[pl.ds(n, fields, stride=nb), :] = part[0:fields]
        place = toff_v[...] * oblocks + oblk_v[...]
        onehot = (iota((SPREAD * oblocks, nb), 0) == jnp.broadcast_to(place, (SPREAD * oblocks, nb))).astype(F32)
        onehot = onehot.astype(BF16)
        hi, lo = split2(contrib[...])
        for k in range(fields):
            r = slice(nb * k, nb * k + nb)
            got = jnp.dot(onehot, hi[r], preferred_element_type=F32) + jnp.dot(
                onehot, lo[r], preferred_element_type=F32
            )
            dense[:, k * LANES : (k + 1) * LANES] = got
        sends = []
        for d in range(SPREAD):
            who = lax.rem(t + d - REACH + tiles, tiles)
            send = pltpu.make_async_remote_copy(
                src_ref=dense.at[pl.ds(d * oblocks, oblocks)],
                dst_ref=recv.at[c * SPREAD + d],
                send_sem=dense_send.at[d],
                recv_sem=dense_recv.at[c * SPREAD + d],
                device_id=(ocean_row, who),
                device_id_type=MESH,
            )
            send.start()
            sends.append(send)
        for send in sends:
            send.wait_send()

    @pl.when(is_ocean)
    def _():
        total = None
        for slot in range((comps - 1) * SPREAD):
            pltpu.make_async_remote_copy(
                src_ref=dense.at[pl.ds(0, oblocks)],
                dst_ref=recv.at[slot],
                send_sem=dense_send.at[0],
                recv_sem=dense_recv.at[slot],
                device_id=(c, t),
                device_id_type=MESH,
            ).wait_recv()
            total = recv[slot] if total is None else total + recv[slot]
        land = mask_v[...].astype(F32)
        rx[...] = total * jnp.concatenate([land] * fields, axis=1)
        for k in range(fields):
            for o in range(oblocks):
                cols = slice(o * LANES, (o + 1) * LANES)
                out[k * lev : k * lev + 1, cols] += rx[o : o + 1, k * LANES : (k + 1) * LANES]


def solution(mesh):
    comps, tiles = mesh.shape["comp"], mesh.shape["tile"]

    def local(column_state, mixing, vertical, flux_coef, atm_block, ocean_block, tile_offset, remap_weights, ocean_mask):
        fields, lev, cells = column_state.shape[2:]
        nb = remap_weights.shape[2]
        rows = fields * lev
        oblocks = cells // LANES
        dims = (fields, lev, cells, comps, tiles, nb)
        result = pl.pallas_call(
            functools.partial(kernel, dims),
            out_shape=jax.ShapeDtypeStruct((rows, cells), F32),
            in_specs=[pl.BlockSpec(memory_space=pl.ANY)] * 9,
            out_specs=pl.BlockSpec(memory_space=pltpu.VMEM),
            scratch_shapes=[
                pltpu.VMEM((rows, cells + 2 * LANES), F32),
                pltpu.VMEM(mixing.shape, F32),
                pltpu.VMEM(vertical.shape, F32),
                pltpu.VMEM(flux_coef.shape, F32),
                pltpu.SMEM((nb,), jnp.int32),
                pltpu.VMEM((1, nb), jnp.int32),
                pltpu.VMEM((1, nb), jnp.int32),
                pltpu.VMEM((nb, LANES, LANES), BF16),
                pltpu.VMEM((oblocks, LANES), jnp.int32),
                pltpu.VMEM((3, rows, LANES), F32),
                pltpu.VMEM((2 * (rows + SURF), rows), BF16),
                pltpu.VMEM((2, 8, LANES), F32),
                pltpu.VMEM((2, 8, LANES), F32),
                pltpu.VMEM((oblocks, 8, LANES), F32),
                pltpu.VMEM((fields * nb, LANES), F32),
                pltpu.VMEM((SPREAD * oblocks, fields * LANES), F32),
                pltpu.VMEM(((comps - 1) * SPREAD, oblocks, fields * LANES), F32),
                pltpu.VMEM((oblocks, fields * LANES), F32),
                pltpu.SemaphoreType.DMA((11,)),
                pltpu.SemaphoreType.DMA((2,)),
                pltpu.SemaphoreType.DMA((2,)),
                pltpu.SemaphoreType.DMA((SPREAD,)),
                pltpu.SemaphoreType.DMA(((comps - 1) * SPREAD,)),
            ],
            compiler_params=pltpu.CompilerParams(collective_id=0, has_side_effects=True),
            name="step",
        )(
            column_state.reshape(rows, cells),
            mixing,
            vertical,
            flux_coef,
            atm_block.reshape(nb),
            ocean_block.reshape(1, nb),
            tile_offset.reshape(1, nb),
            remap_weights.reshape(remap_weights.shape[2:]),
            ocean_mask.reshape(oblocks, LANES),
        )
        return result.reshape(column_state.shape)

    placed = (
        P("comp", "tile", None, None, None),
        P(),
        P(),
        P(),
        P("comp", "tile", None),
        P("comp", "tile", None),
        P("comp", "tile", None),
        P("comp", "tile", None, None, None),
        P("tile", None),
    )
    return jax.shard_map(
        local,
        mesh=mesh,
        in_specs=placed,
        out_specs=P("comp", "tile", None, None, None),
        check_vma=False,
    )
```

time: 76.9 us -> 27.5 us (0.36)
  the two profiles are of different devices: /device:TPU:5 before, /device:TPU:17 now
where the time goes in v1:
time: 27.5 us; the launch traced here: 27.3 us
  Pallas kernels  25.4 us (92%)
  local copies, waits for them, and re-layouts  1.87 us (7%)
    pallas_call x1, Pallas kernels, local(): pl.pallas_call(functools.partial(kernel, dims), out_shape=jax.ShapeDtypeS...  25.4 us
    unnamed x1, local copies, waits for them, and re-layouts  1.87 us

profile of v1, /device:TPU:17, one launch (start us, length us, event | category | flops | bytes accessed | tf_op | source)
XLA Modules:
  0.0 27.3 jit_solution(14418915726096547797)
XLA Ops:
  0.0 25.4 %step.1 = f32[64,2048]{1,0:T(8,128)} custom-call(f32[64,2048]{1,0:T(8,128)} %bitcast.8, f32[2,4,16]{2,1,0:T(4,128)} %mixing.1, f32[2,16,16]{2,1,0:T(8,128)} %vertical.1, f32[2,4]{1,0:T(2,128)} %flux.1, s32[16]{0:T(128)} %bitcast.11, s32[1,16]{1,0:T(1,128)} %bitcast.12, s32[1,16]{1,0:T(1,128)} %bitcast.13, bf16[16,128,128]{2,1,0:T(8,128)(2,1)} %bitcast.9, ...), custom_call_target="tpu_custom_call" | custom-call | tf_op jit(solution)/shard_map/step/pallas_call | solution.py:301
  25.4 1.9 %copy.11 = f32[1,1,4,16,2048]{4,3,2,1,0:T(8,128)} copy(f32[1,1,4,16,2048]{4,3,2,1,0:T(8,128)} %bitcast.7) | data formatting | bytes 1048576

commit v2 on v1

--- a/solution.py
+++ b/solution.py
@@ -12,6 +12,7 @@
 MESH = pl.DeviceIdType.MESH
 F32 = jnp.float32
 BF16 = jnp.bfloat16
+GREET = (-3, -1, 1, 3)
 LANES = 128
 SURF = 16
 
@@ -109,7 +110,7 @@
     @pl.when(is_ocean)
     def _():
         for src in range(comps - 1):
-            for d in range(-REACH, REACH + 1):
+            for d in GREET:
                 who = lax.rem(t - d + tiles, tiles)
                 pl.semaphore_signal(barrier, inc=1, device_id=(src, who), device_id_type=MESH)
 
@@ -157,26 +158,6 @@
     opmat[high : 2 * high] = sq_lo
     half = jnp.where(is_atmos, 0.5, 0.0)
 
-    pl.semaphore_wait(barrier, jnp.where(is_atmos, 2 + SPREAD, 2))
-    to_right = pltpu.make_async_remote_copy(
-        src_ref=pack.at[1],
-        dst_ref=halo.at[0],
-        send_sem=halo_send.at[0],
-        recv_sem=halo_recv.at[0],
-        device_id=(c, right),
-        device_id_type=MESH,
-    )
-    to_left = pltpu.make_async_remote_copy(
-        src_ref=pack.at[0],
-        dst_ref=halo.at[1],
-        send_sem=halo_send.at[1],
-        recv_sem=halo_recv.at[1],
-        device_id=(c, left),
-        device_id_type=MESH,
-    )
-    to_right.start()
-    to_left.start()
-
     def stencil(x, i):
         n = x.shape[1]
         s = slice(8 * i, 8 * i + 8)
@@ -211,6 +192,26 @@
         x = f[8 * i : 8 * i + 8, LANES : LANES + cells]
         y = stencil(x, i)
         out[8 * i : 8 * i + 8, LANES : cells - LANES] = y[:, LANES : cells - LANES]
+    pl.semaphore_wait(barrier, jnp.where(is_atmos, 2 + len(GREET), 2))
+    to_right = pltpu.make_async_remote_copy(
+        src_ref=pack.at[1],
+        dst_ref=halo.at[0],
+        send_sem=halo_send.at[0],
+        recv_sem=halo_recv.at[0],
+        device_id=(c, right),
+        device_id_type=MESH,
+    )
+    to_left = pltpu.make_async_remote_copy(
+        src_ref=pack.at[0],
+        dst_ref=halo.at[1],
+        send_sem=halo_send.at[1],
+        recv_sem=halo_recv.at[1],
+        device_id=(c, left),
+        device_id_type=MESH,
+    )
+    to_right.start()
+    to_left.start()
+
     for j in range(LANES, cells - LANES, 2 * LANES):
         mix(out[:, j : j + 2 * LANES], (j // LANES, j // LANES + 1))
 
@@ -252,13 +253,18 @@
                 onehot, lo[r], preferred_element_type=F32
             )
             dense[:, k * LANES : (k + 1) * LANES] = got
+        spin = lax.rem(t, 4)
         sends = []
-        for d in range(SPREAD):
+        for step in range(SPREAD):
+            if step < REACH:
+                d = REACH + 1 + lax.rem(step + 2 * REACH - spin, REACH)
+            else:
+                d = SPREAD - 1 - step
             who = lax.rem(t + d - REACH + tiles, tiles)
             send = pltpu.make_async_remote_copy(
                 src_ref=dense.at[pl.ds(d * oblocks, oblocks)],
                 dst_ref=recv.at[c * SPREAD + d],
-                send_sem=dense_send.at[d],
+                send_sem=dense_send.at[step],
                 recv_sem=dense_recv.at[c * SPREAD + d],
                 device_id=(ocean_row, who),
                 device_id_type=MESH,
@@ -271,7 +277,7 @@
     @pl.when(is_ocean)
     def _():
         total = None
-        for slot in range((comps - 1) * SPREAD):
+        for slot in sorted(range((comps - 1) * SPREAD), key=lambda slot: slot % SPREAD):
             pltpu.make_async_remote_copy(
                 src_ref=dense.at[pl.ds(0, oblocks)],
                 dst_ref=recv.at[slot],
@@ -300,7 +306,7 @@
         dims = (fields, lev, cells, comps, tiles, nb)
         result = pl.pallas_call(
             functools.partial(kernel, dims),
-            out_shape=jax.ShapeDtypeStruct((rows, cells), F32),
+            out_shape=pltpu.VMEM((rows, cells), F32),
             in_specs=[pl.BlockSpec(memory_space=pl.ANY)] * 9,
             out_specs=pl.BlockSpec(memory_space=pltpu.VMEM),
             scratch_shapes=[

time: 27.5 us -> 25.3 us (0.920)
  local copies, waits for them, and re-layouts: 1.87 us -> 0.8 us
  Pallas kernels: 25.4 us -> 24.4 us
    unnamed x1, local copies, waits for them, and re-layouts: 1.87 us -> 0.8 us
    pallas_call x1, Pallas kernels: 25.4 us -> 24.4 us  [local(): pl.pallas_call(functools.partial(kernel, dims), out_shape=pltpu.VMEM((row...]
where the time goes in v2:
time: 25.3 us; the launch traced here: 25.2 us
  Pallas kernels  24.4 us (96%)
  local copies, waits for them, and re-layouts  0.8 us (3%)
    pallas_call x1, Pallas kernels, local(): pl.pallas_call(functools.partial(kernel, dims), out_shape=pltpu.VMEM((row...  24.4 us
    unnamed x1, local copies, waits for them, and re-layouts  0.8 us

profile of v2, /device:TPU:17, one launch (start us, length us, event | category | flops | bytes accessed | tf_op | source)
XLA Modules:
  0.0 25.2 jit_solution(8019223154593415941)
XLA Ops:
  0.0 24.4 %step.1 = f32[64,2048]{1,0:T(8,128)S(1)} custom-call(f32[64,2048]{1,0:T(8,128)} %bitcast.8, f32[2,4,16]{2,1,0:T(4,128)} %mixing.1, f32[2,16,16]{2,1,0:T(8,128)} %vertical.1, f32[2,4]{1,0:T(2,128)} %flux.1, s32[16]{0:T(128)} %bitcast.11, s32[1,16]{1,0:T(1,128)} %bitcast.12, s32[1,16]{1,0:T(1,128)} %bitcast.13, bf16[16,128,128]{2,1,0:T(8,128)(2,1)} %bitcast.9, ...), custom_call_target="tpu_custom_call" | custom-call | tf_op jit(solution)/shard_map/step/pallas_call | solution.py:307
  24.4 0.8 %copy.11 = f32[1,1,4,16,2048]{4,3,2,1,0:T(8,128)} copy(f32[1,1,4,16,2048]{4,3,2,1,0:T(8,128)S(1)} %bitcast.7) | data formatting | bytes 1048576

commit v3 on v2

--- a/solution.py
+++ b/solution.py
@@ -12,9 +12,11 @@
 MESH = pl.DeviceIdType.MESH
 F32 = jnp.float32
 BF16 = jnp.bfloat16
-GREET = (-3, -1, 1, 3)
+HALF = 4
+PLANE = 8
 LANES = 128
 SURF = 16
+GROUP = 16
 
 
 def iota(shape, dim):
@@ -62,12 +64,17 @@
     contrib,
     dense,
     recv,
+    relay,
+    packed_ops,
     rx,
     load_sem,
     halo_send,
     halo_recv,
+    relay_send,
+    relay_recv,
     dense_send,
     dense_recv,
+    known,
 ):
     fields, lev, cells, comps, tiles, nb = dims
     rows = fields * lev
@@ -102,61 +109,104 @@
         pltpu.make_async_copy(mask, mask_v, load_sem.at[10]),
     ]
     barrier = pltpu.get_barrier_semaphore()
-    for who in (left, right):
-        pl.semaphore_signal(barrier, inc=1, device_id=(c, who), device_id_type=MESH)
+    spot = lax.rem(t, PLANE)
+    first_spot = spot == 0
+    last_spot = spot == PLANE - 1
+
+    def greet(row, who):
+        pl.semaphore_signal(barrier, inc=1, device_id=(row, lax.rem(who + tiles, tiles)), device_id_type=MESH)
+
+    greet(c, t - 1)
+
+    @pl.when(jnp.logical_not(last_spot))
+    def _():
+        greet(c, t + 1)
+
+    @pl.when(last_spot)
+    def _():
+        greet(c, t + PLANE)
+        greet(c, t - PLANE + 1)
+
     for load in loads:
         load.start()
 
+    @pl.when(is_atmos)
+    def _():
+        for d in range(1, REACH + 1):
+
+            @pl.when(spot < d)
+            def _():
+                greet(ocean_row, t - d)
+
     @pl.when(is_ocean)
     def _():
-        for src in range(comps - 1):
-            for d in GREET:
-                who = lax.rem(t - d + tiles, tiles)
-                pl.semaphore_signal(barrier, inc=1, device_id=(src, who), device_id_type=MESH)
+        for d in range(-REACH, REACH + 1):
+            there = spot - d
+            wanted = (there < HALF) & (there >= 0) if d else spot < PLANE
+            if d > 0:
+                wanted = wanted | (there < 0)
+
+            @pl.when(wanted)
+            def _():
+                for src in range(comps - 1):
+                    greet(src, t - d)
 
     loads[0].wait()
     loads[1].wait()
     lane = iota((8, LANES), 1)
+    sub = iota((8, LANES), 0)
+    place_in = lane % GROUP
     groups = rows // 8
-    first = jnp.zeros((8, LANES), F32)
-    last = jnp.zeros((8, LANES), F32)
+    packed = jnp.zeros((8, LANES), F32)
     for i in range(groups):
-        here = lane // 2 == i
+        here = lane // GROUP == i
         a = f[8 * i : 8 * i + 8, LANES : 2 * LANES]
         b = f[8 * i : 8 * i + 8, cells : cells + LANES]
-        first = jnp.where(here, pltpu.roll(a, 2 * i, 1) if i else a, first)
-        last = jnp.where(here, pltpu.roll(b, 2 * i + 2, 1), last)
-    pack[0] = first
-    pack[1] = last
+        packed = jnp.where(here & (place_in < 7), pltpu.roll(a, GROUP * i + 2, 1), packed)
+        packed = jnp.where(here & (place_in >= 7), pltpu.roll(b, (GROUP * i + 12) % LANES, 1), packed)
+    pack[...] = packed
 
     loads[3].wait()
     loads[4].wait()
     loads[5].wait()
-    mix_g = mix_v[group]
-    rates = jnp.concatenate([column(mix_g[k : k + 1, :], lev) for k in range(fields)], axis=0)
+    def rate_column(mix_g):
+        return jnp.concatenate([column(mix_g[k : k + 1, :], lev) for k in range(fields)], axis=0)
+
+    rates = rate_column(mix_v[group])
     keep = 1.0 - 2.0 * rates
     coef[0] = jnp.broadcast_to(keep * keep + 2.0 * rates * rates, (rows, LANES))
     coef[1] = jnp.broadcast_to(2.0 * rates * keep, (rows, LANES))
     coef[2] = jnp.broadcast_to(rates * rates, (rows, LANES))
-    ver_g = ver_v[group]
-    spread_l = (lax.rem(iota((rows, lev), 0), lev) == iota((rows, lev), 1)).astype(F32)
-    spread_r = (lax.rem(iota((lev, rows), 1), lev) == iota((lev, rows), 0)).astype(F32)
-    hp = lax.Precision.HIGHEST
-    tall = jnp.dot(spread_l, ver_g, precision=hp, preferred_element_type=F32)
-    square = jnp.dot(tall, spread_r, precision=hp, preferred_element_type=F32)
-    square = jnp.where(iota((rows, rows), 0) // lev == iota((rows, rows), 1) // lev, square, 0.0)
+    spread = (lax.rem(iota((lev, rows), 1), lev) == iota((lev, rows), 0)).astype(F32)
+    stacked = jnp.concatenate([ver_v[group]] * fields + [ver_v[group][lev - 8 : lev]], axis=0)
+    wide = jnp.dot(stacked, spread, precision=lax.Precision.HIGHEST, preferred_element_type=F32)
+    square = jnp.where(iota((rows, rows), 0) // lev == iota((rows, rows), 1) // lev, wide[0:rows], 0.0)
     fa = jnp.concatenate([column(flux_v[0:1, :], fields), jnp.zeros((SURF - fields, 1), F32)], axis=0)
     fb = jnp.concatenate([column(flux_v[1:2, :], fields), jnp.zeros((SURF - fields, 1), F32)], axis=0)
     who_row, who_col = iota((SURF, rows), 0), iota((SURF, rows), 1)
-    pick = jnp.where(who_col == who_row * lev + lev - 1, fa, 0.0) + jnp.where(
-        who_col == who_row * lev + lev - 2, fb, 0.0
-    )
-    linear = pick + jnp.dot(pick, square, precision=hp, preferred_element_type=F32)
+    level = who_col % lev
+    top = jnp.where(level == lev - 1, 1.0, 0.0) + wide[rows + 7 : rows + 8]
+    under = jnp.where(level == lev - 2, 1.0, 0.0) + wide[rows + 6 : rows + 7]
+    linear = jnp.where(who_col // lev == who_row, fa * top + fb * under, 0.0)
     high = rows + SURF
     sq_hi, sq_lo = split2(jnp.concatenate([square, linear], axis=0))
     opmat[0:high] = sq_hi
     opmat[high : 2 * high] = sq_lo
     half = jnp.where(is_atmos, 0.5, 0.0)
+
+    def packed_column(v):
+        got = jnp.zeros((8, LANES), F32)
+        for i in range(groups):
+            got = jnp.where(lane // GROUP == i, jnp.broadcast_to(v[8 * i : 8 * i + 8], (8, LANES)), got)
+        return got
+
+    pr = packed_column(rates)
+    pk = 1.0 - 2.0 * pr
+    lin = packed_column(column(jnp.sum(linear, axis=0, keepdims=True), rows))
+    packed_ops[0] = pk * pk + 2.0 * pr * pr
+    packed_ops[1] = 2.0 * pr * pk
+    packed_ops[2] = pr * pr
+    packed_ops[3] = lin
 
     def stencil(x, i):
         n = x.shape[1]
@@ -166,7 +216,7 @@
         far = pltpu.roll(x, 2, 1) + pltpu.roll(x, n - 2, 1)
         return wide(coef[0, s]) * x + wide(coef[1, s]) * near + wide(coef[2, s]) * far
 
-    def mix(x, spots):
+    def mix(x, spots, store_surface):
         hi, lo = split2(x)
         p = jnp.dot(opmat[...], hi, preferred_element_type=F32)
         q = jnp.dot(opmat[0:high], lo, preferred_element_type=F32)
@@ -177,102 +227,218 @@
             cols = slice(b * LANES, (b + 1) * LANES)
             part = slice(i * LANES, (i + 1) * LANES)
             s = flux_now[:, part]
-            surf[b] = s
+            if store_surface:
+                kept = s
+                if b == 0:
+                    kept = jnp.where((sub < fields) & (lane < 2), 0.0, kept)
+                    kept = jnp.where((sub >= 4) & (sub < 6) & (lane == sub - 4), 1.0, kept)
+                if b == ntile - 1:
+                    kept = jnp.where((sub < fields) & (lane >= LANES - 2), 0.0, kept)
+                    kept = jnp.where((sub >= 6) & (lane == LANES - 8 + sub), 1.0, kept)
+                surf[b] = kept
             for k in range(fields):
                 base = k * lev
                 out[base : base + lev - 8, cols] = mixed[base : base + lev - 8, part]
                 moved = pltpu.roll(s, 7 - k, 0)
-                low = iota((8, LANES), 0) == 7
+                low = sub == 7
                 out[base + lev - 8 : base + lev, cols] = mixed[base + lev - 8 : base + lev, part] - jnp.where(
                     low, half * moved, 0.0
                 )
 
     loads[2].wait()
     for i in range(groups):
-        x = f[8 * i : 8 * i + 8, LANES : LANES + cells]
-        y = stencil(x, i)
-        out[8 * i : 8 * i + 8, LANES : cells - LANES] = y[:, LANES : cells - LANES]
-    pl.semaphore_wait(barrier, jnp.where(is_atmos, 2 + len(GREET), 2))
-    to_right = pltpu.make_async_remote_copy(
-        src_ref=pack.at[1],
-        dst_ref=halo.at[0],
-        send_sem=halo_send.at[0],
-        recv_sem=halo_recv.at[0],
-        device_id=(c, right),
-        device_id_type=MESH,
+        s = slice(8 * i, 8 * i + 8)
+        out[s, :] = stencil(f[s, LANES : LANES + cells], i)
+    pl.semaphore_wait(
+        barrier,
+        jnp.where(last_spot, 3, 2) + jnp.where(
+            is_atmos,
+            jnp.where(spot < HALF, spot + 1 + REACH, 1 + jnp.maximum(spot - (PLANE - 1 - REACH), 0)),
+            (comps - 1) * jnp.maximum(spot - (PLANE - 1 - REACH), 0),
+        ),
     )
-    to_left = pltpu.make_async_remote_copy(
-        src_ref=pack.at[0],
-        dst_ref=halo.at[1],
-        send_sem=halo_send.at[1],
-        recv_sem=halo_recv.at[1],
-        device_id=(c, left),
-        device_id_type=MESH,
-    )
+
+    def pack_copy(way, src, dst, send, recv_at, who):
+        return pltpu.make_async_remote_copy(
+            src_ref=src,
+            dst_ref=dst,
+            send_sem=send,
+            recv_sem=recv_at,
+            device_id=(c, lax.rem(who + tiles, tiles)),
+            device_id_type=MESH,
+        )
+
+    to_right = pack_copy(0, pack, halo.at[0], halo_send.at[0], halo_recv.at[0], t + 1)
+    to_left = pack_copy(1, pack, halo.at[1], halo_send.at[1], halo_recv.at[1], t - 1)
+    to_relay = pack_copy(1, pack, relay, relay_send.at[0], relay_recv.at[0], t + PLANE - 1)
+    onward = pack_copy(1, relay, halo.at[1], relay_send.at[1], halo_recv.at[1], t - PLANE)
+
     to_right.start()
-    to_left.start()
-
-    for j in range(LANES, cells - LANES, 2 * LANES):
-        mix(out[:, j : j + 2 * LANES], (j // LANES, j // LANES + 1))
-
-    to_right.wait()
-    to_left.wait()
+
+    @pl.when(is_ocean)
+    def _():
+        for d in range(1, REACH + 1):
+
+            @pl.when(spot + d >= PLANE)
+            def _():
+                for src in range(comps - 1):
+                    who = (src, lax.rem(t + d, tiles))
+                    pl.semaphore_signal(known.at[4], inc=1, device_id=who, device_id_type=MESH)
+
+    @pl.when(jnp.logical_not(first_spot))
+    def _():
+        to_left.start()
+
+    @pl.when(first_spot)
+    def _():
+        to_relay.start()
+
+    @pl.when(last_spot)
+    def _():
+        to_relay.wait_recv()
+        onward.start()
+
+    for j in range(0, cells, 2 * LANES):
+        mix(out[:, j : j + 2 * LANES], (j // LANES, j // LANES + 1), True)
+    loads[6].wait()
+    loads[7].wait()
+    loads[8].wait()
+    loads[9].wait()
+    loads[10].wait()
+
+    @pl.when(is_atmos)
+    def _():
+        for n in range(nb):
+            picked = surf[ablk_s[n]].astype(BF16)
+            part = jnp.dot(picked, w_v[n], preferred_element_type=F32)
+            contrib[pl.ds(n, 8, stride=nb), :] = part
+
+    to_right.wait_recv()
+    to_left.wait_recv()
+
+    def dense_copy(d):
+        return pltpu.make_async_remote_copy(
+            src_ref=dense.at[pl.ds((d + REACH) * oblocks, oblocks)],
+            dst_ref=recv.at[c * SPREAD + d + REACH],
+            send_sem=dense_send.at[d + REACH],
+            recv_sem=dense_recv.at[c * SPREAD + d + REACH],
+            device_id=(ocean_row, lax.rem(t + d + tiles, tiles)),
+            device_id_type=MESH,
+        )
+
+    @pl.when(is_atmos)
+    def _():
+        x = jnp.where(place_in < 2, pltpu.roll(halo[0], LANES - 10, 1), pack[...])
+        x = jnp.where(place_in >= 12, pltpu.roll(halo[1], 10, 1), x)
+        near = pltpu.roll(x, 1, 1) + pltpu.roll(x, LANES - 1, 1)
+        far = pltpu.roll(x, 2, 1) + pltpu.roll(x, LANES - 2, 1)
+        z = packed_ops[3] * (packed_ops[0] * x + packed_ops[1] * near + packed_ops[2] * far)
+        for shift in (4, 2, 1):
+            z = z + pltpu.roll(z, shift, 0)
+        z = z + pltpu.roll(z, LANES - GROUP, 1)
+        r = jnp.tanh(z).astype(BF16).astype(F32)
+        place = toff_v[...] * oblocks + oblk_v[...]
+        onehot = (iota((SPREAD * oblocks, nb), 0) == jnp.broadcast_to(place, (SPREAD * oblocks, nb))).astype(F32)
+        onehot = onehot.astype(BF16)
+        for k in range(fields):
+            got = contrib[nb * k : nb * k + nb, :]
+            for e, p in enumerate((2, 3, 10, 11)):
+                at = 2 * k * GROUP + p
+                scale = jnp.broadcast_to(r[:, at : at + 1], (8, LANES))
+                scale = jnp.concatenate([scale] * (nb // 8), axis=0)
+                got = got + scale * contrib[nb * (4 + e) : nb * (5 + e), :]
+            hi, lo = split2(got)
+            dense[:, k * LANES : (k + 1) * LANES] = jnp.dot(onehot, hi, preferred_element_type=F32) + jnp.dot(
+                onehot, lo, preferred_element_type=F32
+            )
+        for d in range(1, REACH + 1):
+
+            @pl.when(spot + d >= PLANE)
+            def _():
+                dense_copy(d).start()
+
+        def inside(d):
+            return (spot + d >= 0) & (spot + d < PLANE)
+
+        def send(d, wanted):
+            @pl.when(wanted)
+            def _():
+                dense_copy(d).start()
+
+        def tell(stage, who, wanted):
+            @pl.when(wanted)
+            def _():
+                pl.semaphore_signal(known.at[stage], inc=1, device_id=(c, who), device_id_type=MESH)
+
+        upper = spot >= HALF
+        tell(0, right, (spot >= HALF - 1) & (spot < PLANE - 1))
+        tell(1, left, (spot == HALF + 1) | (spot == HALF + 2))
+        for d in (0, -1, 1):
+            send(d, inside(d))
+        for d in (-2, 2, -3, 3):
+            send(d, inside(d) & jnp.logical_not(upper))
+
+        @pl.when(spot < REACH)
+        def _():
+            pl.semaphore_wait(known.at[4], REACH - spot)
+            for d in range(1, REACH + 1):
+                send(-d, spot < d)
+
+        @pl.when(upper)
+        def _():
+            pl.semaphore_wait(known.at[0], 1)
+            tell(2, right, spot < PLANE - 1)
+            dense_copy(-2).start()
+
+            @pl.when(spot < HALF + 2)
+            def _():
+                pl.semaphore_wait(known.at[1], 1)
+                tell(3, left, spot == HALF + 1)
+                dense_copy(2).start()
+
+            @pl.when(spot > HALF)
+            def _():
+                pl.semaphore_wait(known.at[2], 1)
+
+            dense_copy(-3).start()
+
+            @pl.when(spot == HALF)
+            def _():
+                pl.semaphore_wait(known.at[3], 1)
+                dense_copy(3).start()
+
     hl = halo[0]
     hr = halo[1]
     for i in range(groups):
         s = slice(8 * i, 8 * i + 8)
-        f[s, 0:LANES] = pltpu.roll(hl, LANES - 2 * i - 2, 1)
-        f[s, LANES + cells : 2 * LANES + cells] = pltpu.roll(hr, LANES - 2 * i, 1) if i else hr
+        f[s, 0:LANES] = pltpu.roll(hl, (116 - GROUP * i) % LANES, 1)
+        f[s, LANES + cells : 2 * LANES + cells] = pltpu.roll(hr, 126 - GROUP * i, 1)
     lefts, rights = [], []
     for i in range(groups):
         s = slice(8 * i, 8 * i + 8)
         lefts.append(stencil(f[s, 0 : 3 * LANES], i)[:, LANES : 2 * LANES])
         rights.append(stencil(f[s, cells - LANES : cells + 2 * LANES], i)[:, LANES : 2 * LANES])
     edge = jnp.concatenate([jnp.concatenate(lefts, axis=0), jnp.concatenate(rights, axis=0)], axis=1)
-    mix(edge, (0, ntile - 1))
-
-    loads[6].wait()
-    loads[7].wait()
-    loads[8].wait()
-    loads[9].wait()
-    loads[10].wait()
+    mix(edge, (0, ntile - 1), False)
+
+    to_right.wait_send()
+
+    @pl.when(jnp.logical_not(first_spot))
+    def _():
+        to_left.wait_send()
+
+    @pl.when(first_spot)
+    def _():
+        to_relay.wait_send()
+
+    @pl.when(last_spot)
+    def _():
+        onward.wait_send()
 
     @pl.when(is_atmos)
     def _():
-        for n in range(nb):
-            picked = surf[ablk_s[n]].astype(BF16)
-            part = jnp.dot(picked, w_v[n], preferred_element_type=F32)
-            contrib[pl.ds(n, fields, stride=nb), :] = part[0:fields]
-        place = toff_v[...] * oblocks + oblk_v[...]
-        onehot = (iota((SPREAD * oblocks, nb), 0) == jnp.broadcast_to(place, (SPREAD * oblocks, nb))).astype(F32)
-        onehot = onehot.astype(BF16)
-        hi, lo = split2(contrib[...])
-        for k in range(fields):
-            r = slice(nb * k, nb * k + nb)
-            got = jnp.dot(onehot, hi[r], preferred_element_type=F32) + jnp.dot(
-                onehot, lo[r], preferred_element_type=F32
-            )
-            dense[:, k * LANES : (k + 1) * LANES] = got
-        spin = lax.rem(t, 4)
-        sends = []
-        for step in range(SPREAD):
-            if step < REACH:
-                d = REACH + 1 + lax.rem(step + 2 * REACH - spin, REACH)
-            else:
-                d = SPREAD - 1 - step
-            who = lax.rem(t + d - REACH + tiles, tiles)
-            send = pltpu.make_async_remote_copy(
-                src_ref=dense.at[pl.ds(d * oblocks, oblocks)],
-                dst_ref=recv.at[c * SPREAD + d],
-                send_sem=dense_send.at[step],
-                recv_sem=dense_recv.at[c * SPREAD + d],
-                device_id=(ocean_row, who),
-                device_id_type=MESH,
-            )
-            send.start()
-            sends.append(send)
-        for send in sends:
-            send.wait_send()
+        for d in range(-REACH, REACH + 1):
+            dense_copy(d).wait_send()
 
     @pl.when(is_ocean)
     def _():
@@ -321,18 +487,23 @@
                 pltpu.VMEM((oblocks, LANES), jnp.int32),
                 pltpu.VMEM((3, rows, LANES), F32),
                 pltpu.VMEM((2 * (rows + SURF), rows), BF16),
-                pltpu.VMEM((2, 8, LANES), F32),
+                pltpu.VMEM((8, LANES), F32),
                 pltpu.VMEM((2, 8, LANES), F32),
                 pltpu.VMEM((oblocks, 8, LANES), F32),
-                pltpu.VMEM((fields * nb, LANES), F32),
+                pltpu.VMEM((8 * nb, LANES), F32),
                 pltpu.VMEM((SPREAD * oblocks, fields * LANES), F32),
                 pltpu.VMEM(((comps - 1) * SPREAD, oblocks, fields * LANES), F32),
+                pltpu.VMEM((8, LANES), F32),
+                pltpu.VMEM((4, 8, LANES), F32),
                 pltpu.VMEM((oblocks, fields * LANES), F32),
                 pltpu.SemaphoreType.DMA((11,)),
                 pltpu.SemaphoreType.DMA((2,)),
                 pltpu.SemaphoreType.DMA((2,)),
+                pltpu.SemaphoreType.DMA((2,)),
+                pltpu.SemaphoreType.DMA((1,)),
                 pltpu.SemaphoreType.DMA((SPREAD,)),
                 pltpu.SemaphoreType.DMA(((comps - 1) * SPREAD,)),
+                pltpu.SemaphoreType.REGULAR((5,)),
             ],
             compiler_params=pltpu.CompilerParams(collective_id=0, has_side_effects=True),
             name="step",

time: 25.3 us -> 24.1 us (0.953)
  Pallas kernels: 24.4 us -> 23.1 us
    pallas_call x1, Pallas kernels: 24.4 us -> 23.1 us  [local(): pl.pallas_call(functools.partial(kernel, dims), out_shape=pltpu.VMEM((row...]
where the time goes in v3:
time: 24.1 us; the launch traced here: 24 us
  Pallas kernels  23.1 us (96%)
  local copies, waits for them, and re-layouts  0.8 us (3%)
    pallas_call x1, Pallas kernels, local(): pl.pallas_call(functools.partial(kernel, dims), out_shape=pltpu.VMEM((row...  23.1 us
    unnamed x1, local copies, waits for them, and re-layouts  0.8 us

profile of v3, /device:TPU:17, one launch (start us, length us, event | category | flops | bytes accessed | tf_op | source)
XLA Modules:
  0.0 24.0 jit_solution(4143408820374464182)
XLA Ops:
  0.0 23.1 %step.1 = f32[64,2048]{1,0:T(8,128)S(1)} custom-call(f32[64,2048]{1,0:T(8,128)} %bitcast.8, f32[2,4,16]{2,1,0:T(4,128)} %mixing.1, f32[2,16,16]{2,1,0:T(8,128)} %vertical.1, f32[2,4]{1,0:T(2,128)} %flux.1, s32[16]{0:T(128)} %bitcast.11, s32[1,16]{1,0:T(1,128)} %bitcast.12, s32[1,16]{1,0:T(1,128)} %bitcast.13, bf16[16,128,128]{2,1,0:T(8,128)(2,1)} %bitcast.9, ...), custom_call_target="tpu_custom_call" | custom-call | tf_op jit(solution)/shard_map/step/pallas_call | solution.py:473
  23.2 0.8 %copy.11 = f32[1,1,4,16,2048]{4,3,2,1,0:T(8,128)} copy(f32[1,1,4,16,2048]{4,3,2,1,0:T(8,128)S(1)} %bitcast.7) | data formatting | bytes 1048576

commit v4 on v3

--- a/solution.py
+++ b/solution.py
@@ -110,21 +110,19 @@
     ]
     barrier = pltpu.get_barrier_semaphore()
     spot = lax.rem(t, PLANE)
-    first_spot = spot == 0
-    last_spot = spot == PLANE - 1
+    start = t == 0
+    helper = t == PLANE - 1
+    end = t == tiles - 1
 
     def greet(row, who):
         pl.semaphore_signal(barrier, inc=1, device_id=(row, lax.rem(who + tiles, tiles)), device_id_type=MESH)
 
     greet(c, t - 1)
 
-    @pl.when(jnp.logical_not(last_spot))
-    def _():
-        greet(c, t + 1)
-
-    @pl.when(last_spot)
-    def _():
-        greet(c, t + PLANE)
+    greet(c, jnp.where(end, t + PLANE, t + 1))
+
+    @pl.when(helper)
+    def _():
         greet(c, t - PLANE + 1)
 
     for load in loads:
@@ -251,7 +249,7 @@
         out[s, :] = stencil(f[s, LANES : LANES + cells], i)
     pl.semaphore_wait(
         barrier,
-        jnp.where(last_spot, 3, 2) + jnp.where(
+        jnp.where(helper, 3, 2) + jnp.where(
             is_atmos,
             jnp.where(spot < HALF, spot + 1 + REACH, 1 + jnp.maximum(spot - (PLANE - 1 - REACH), 0)),
             (comps - 1) * jnp.maximum(spot - (PLANE - 1 - REACH), 0),
@@ -285,15 +283,15 @@
                     who = (src, lax.rem(t + d, tiles))
                     pl.semaphore_signal(known.at[4], inc=1, device_id=who, device_id_type=MESH)
 
-    @pl.when(jnp.logical_not(first_spot))
+    @pl.when(jnp.logical_not(start))
     def _():
         to_left.start()
 
-    @pl.when(first_spot)
+    @pl.when(start)
     def _():
         to_relay.start()
 
-    @pl.when(last_spot)
+    @pl.when(helper)
     def _():
         to_relay.wait_recv()
         onward.start()
@@ -423,15 +421,15 @@
 
     to_right.wait_send()
 
-    @pl.when(jnp.logical_not(first_spot))
+    @pl.when(jnp.logical_not(start))
     def _():
         to_left.wait_send()
 
-    @pl.when(first_spot)
+    @pl.when(start)
     def _():
         to_relay.wait_send()
 
-    @pl.when(last_spot)
+    @pl.when(helper)
     def _():
         onward.wait_send()
 

time: 24.1 us -> 22.3 us (0.925)
  the two profiles are of different devices: /device:TPU:17 before, /device:TPU:25 now
where the time goes in v4:
time: 22.3 us; the launch traced here: 22.2 us
  Pallas kernels  21.4 us (96%)
  local copies, waits for them, and re-layouts  0.8 us (4%)
    pallas_call x1, Pallas kernels, local(): pl.pallas_call(functools.partial(kernel, dims), out_shape=pltpu.VMEM((row...  21.4 us
    unnamed x1, local copies, waits for them, and re-layouts  0.8 us

profile of v4, /device:TPU:25, one launch (start us, length us, event | category | flops | bytes accessed | tf_op | source)
XLA Modules:
  0.0 22.2 jit_solution(1073646747920053951)
XLA Ops:
  0.0 21.4 %step.1 = f32[64,2048]{1,0:T(8,128)S(1)} custom-call(f32[64,2048]{1,0:T(8,128)} %bitcast.8, f32[2,4,16]{2,1,0:T(4,128)} %mixing.1, f32[2,16,16]{2,1,0:T(8,128)} %vertical.1, f32[2,4]{1,0:T(2,128)} %flux.1, s32[16]{0:T(128)} %bitcast.11, s32[1,16]{1,0:T(1,128)} %bitcast.12, s32[1,16]{1,0:T(1,128)} %bitcast.13, bf16[16,128,128]{2,1,0:T(8,128)(2,1)} %bitcast.9, ...), custom_call_target="tpu_custom_call" | custom-call | tf_op jit(solution)/shard_map/step/pallas_call | solution.py:471
  21.4 0.8 %copy.11 = f32[1,1,4,16,2048]{4,3,2,1,0:T(8,128)} copy(f32[1,1,4,16,2048]{4,3,2,1,0:T(8,128)S(1)} %bitcast.7) | data formatting | bytes 1048576

commit v5 on v4

--- a/solution.py
+++ b/solution.py
@@ -64,12 +64,22 @@
     contrib,
     dense,
     recv,
+    packed_ops,
+    beside,
+    seam,
+    seam_got,
+    seam_pack,
+    seam_r,
     relay,
-    packed_ops,
+    onehot_v,
     rx,
     load_sem,
     halo_send,
     halo_recv,
+    seam_send,
+    seam_recv,
+    pack_send,
+    pack_recv,
     relay_send,
     relay_recv,
     dense_send,
@@ -111,19 +121,26 @@
     barrier = pltpu.get_barrier_semaphore()
     spot = lax.rem(t, PLANE)
     start = t == 0
+    end = t == tiles - 1
+    ocean_start = (t < REACH + 1) | (t >= tiles - REACH)
+    ocean_end = (t < REACH) | (t >= tiles - REACH - 1)
+    near_seam = ocean_start | ocean_end
     helper = t == PLANE - 1
-    end = t == tiles - 1
+    lower = (spot < HALF) | (t < PLANE)
 
     def greet(row, who):
         pl.semaphore_signal(barrier, inc=1, device_id=(row, lax.rem(who + tiles, tiles)), device_id_type=MESH)
 
     greet(c, t - 1)
 
-    greet(c, jnp.where(end, t + PLANE, t + 1))
+    @pl.when(jnp.logical_not(end))
+    def _():
+        greet(c, t + 1)
 
     @pl.when(helper)
     def _():
         greet(c, t - PLANE + 1)
+        greet(c, t - PLANE)
 
     for load in loads:
         load.start()
@@ -136,11 +153,17 @@
             def _():
                 greet(ocean_row, t - d)
 
+        @pl.when(start)
+        def _():
+            greet(ocean_row, t - REACH - 1)
+
     @pl.when(is_ocean)
     def _():
         for d in range(-REACH, REACH + 1):
             there = spot - d
-            wanted = (there < HALF) & (there >= 0) if d else spot < PLANE
+            wanted = (there >= 0) & (there < PLANE)
+            if d:
+                wanted = wanted & ((there < HALF) | (t < PLANE))
             if d > 0:
                 wanted = wanted | (there < 0)
 
@@ -148,6 +171,11 @@
             def _():
                 for src in range(comps - 1):
                     greet(src, t - d)
+
+        @pl.when(t == REACH)
+        def _():
+            for src in range(comps - 1):
+                greet(src, t - REACH - 1)
 
     loads[0].wait()
     loads[1].wait()
@@ -176,7 +204,7 @@
     coef[1] = jnp.broadcast_to(2.0 * rates * keep, (rows, LANES))
     coef[2] = jnp.broadcast_to(rates * rates, (rows, LANES))
     spread = (lax.rem(iota((lev, rows), 1), lev) == iota((lev, rows), 0)).astype(F32)
-    stacked = jnp.concatenate([ver_v[group]] * fields + [ver_v[group][lev - 8 : lev]], axis=0)
+    stacked = jnp.concatenate([ver_v[group]] * fields + [ver_v[0][lev - 8 : lev]], axis=0)
     wide = jnp.dot(stacked, spread, precision=lax.Precision.HIGHEST, preferred_element_type=F32)
     square = jnp.where(iota((rows, rows), 0) // lev == iota((rows, rows), 1) // lev, wide[0:rows], 0.0)
     fa = jnp.concatenate([column(flux_v[0:1, :], fields), jnp.zeros((SURF - fields, 1), F32)], axis=0)
@@ -198,7 +226,7 @@
             got = jnp.where(lane // GROUP == i, jnp.broadcast_to(v[8 * i : 8 * i + 8], (8, LANES)), got)
         return got
 
-    pr = packed_column(rates)
+    pr = packed_column(rate_column(mix_v[0]))
     pk = 1.0 - 2.0 * pr
     lin = packed_column(column(jnp.sum(linear, axis=0, keepdims=True), rows))
     packed_ops[0] = pk * pk + 2.0 * pr * pr
@@ -243,59 +271,112 @@
                     low, half * moved, 0.0
                 )
 
+    pl.semaphore_wait(
+        barrier,
+        jnp.where(end, 3, 2)
+        + jnp.where(
+            is_atmos,
+            jnp.where(lower, 1 + REACH + jnp.minimum(spot, PLANE - 1 - spot), 1)
+            + jnp.maximum(spot - (PLANE - 1 - REACH), 0)
+            + jnp.where(end, 1, 0),
+            (comps - 1) * (jnp.maximum(spot - (PLANE - 1 - REACH), 0) + jnp.where(t == tiles - REACH - 1, 1, 0)),
+        ),
+    )
+
+    def pack_copy(way, who):
+        return pltpu.make_async_remote_copy(
+            src_ref=pack,
+            dst_ref=halo.at[way],
+            send_sem=halo_send.at[way],
+            recv_sem=halo_recv.at[way],
+            device_id=(c, who),
+            device_id_type=MESH,
+        )
+
+    to_right = pack_copy(0, right)
+    to_left = pack_copy(1, left)
+    to_right.start()
+
+    to_relay = pltpu.make_async_remote_copy(
+        src_ref=pack,
+        dst_ref=relay,
+        send_sem=relay_send.at[0],
+        recv_sem=relay_recv.at[0],
+        device_id=(c, PLANE - 1),
+        device_id_type=MESH,
+    )
+    onward = pltpu.make_async_remote_copy(
+        src_ref=relay,
+        dst_ref=halo.at[1],
+        send_sem=relay_send.at[1],
+        recv_sem=halo_recv.at[1],
+        device_id=(c, tiles - 1),
+        device_id_type=MESH,
+    )
+
+    @pl.when(jnp.logical_not(start))
+    def _():
+        to_left.start()
+
+    @pl.when(start)
+    def _():
+        to_relay.start()
+
+    @pl.when(end)
+    def _():
+        pl.semaphore_signal(known.at[5], inc=1, device_id=(c, PLANE - 1), device_id_type=MESH)
+
+    side = jnp.where(end, 1, 0)
+
+    def seam_pack_copy(d):
+        return pltpu.make_async_remote_copy(
+            src_ref=pack,
+            dst_ref=seam_pack.at[2 * c + side],
+            send_sem=pack_send.at[d + REACH + 1],
+            recv_sem=pack_recv.at[2 * c + side],
+            device_id=(ocean_row, lax.rem(t + d + tiles, tiles)),
+            device_id_type=MESH,
+        )
+
+    def seam_copy(d):
+        return pltpu.make_async_remote_copy(
+            src_ref=seam.at[pl.ds((d + REACH) * oblocks, oblocks)],
+            dst_ref=seam_got.at[2 * c + side],
+            send_sem=seam_send.at[d + REACH],
+            recv_sem=seam_recv.at[2 * c + side],
+            device_id=(ocean_row, lax.rem(t + d + tiles, tiles)),
+            device_id_type=MESH,
+        )
+
+    @pl.when(is_atmos & end)
+    def _():
+        for d in range(1, REACH + 2):
+            seam_pack_copy(d).start()
+
+    @pl.when(is_atmos & start)
+    def _():
+        for d in range(0, REACH + 1):
+            seam_pack_copy(d).start()
+
+    @pl.when(is_ocean)
+    def _():
+        for d in range(1, REACH + 1):
+
+            @pl.when(spot + d >= PLANE)
+            def _():
+                for src in range(comps - 1):
+                    who = (src, lax.rem(t + d, tiles))
+                    pl.semaphore_signal(known.at[4], inc=1, device_id=who, device_id_type=MESH)
+
+        @pl.when(t == tiles - REACH - 1)
+        def _():
+            for src in range(comps - 1):
+                pl.semaphore_signal(known.at[4], inc=1, device_id=(src, 0), device_id_type=MESH)
+
     loads[2].wait()
     for i in range(groups):
         s = slice(8 * i, 8 * i + 8)
         out[s, :] = stencil(f[s, LANES : LANES + cells], i)
-    pl.semaphore_wait(
-        barrier,
-        jnp.where(helper, 3, 2) + jnp.where(
-            is_atmos,
-            jnp.where(spot < HALF, spot + 1 + REACH, 1 + jnp.maximum(spot - (PLANE - 1 - REACH), 0)),
-            (comps - 1) * jnp.maximum(spot - (PLANE - 1 - REACH), 0),
-        ),
-    )
-
-    def pack_copy(way, src, dst, send, recv_at, who):
-        return pltpu.make_async_remote_copy(
-            src_ref=src,
-            dst_ref=dst,
-            send_sem=send,
-            recv_sem=recv_at,
-            device_id=(c, lax.rem(who + tiles, tiles)),
-            device_id_type=MESH,
-        )
-
-    to_right = pack_copy(0, pack, halo.at[0], halo_send.at[0], halo_recv.at[0], t + 1)
-    to_left = pack_copy(1, pack, halo.at[1], halo_send.at[1], halo_recv.at[1], t - 1)
-    to_relay = pack_copy(1, pack, relay, relay_send.at[0], relay_recv.at[0], t + PLANE - 1)
-    onward = pack_copy(1, relay, halo.at[1], relay_send.at[1], halo_recv.at[1], t - PLANE)
-
-    to_right.start()
-
-    @pl.when(is_ocean)
-    def _():
-        for d in range(1, REACH + 1):
-
-            @pl.when(spot + d >= PLANE)
-            def _():
-                for src in range(comps - 1):
-                    who = (src, lax.rem(t + d, tiles))
-                    pl.semaphore_signal(known.at[4], inc=1, device_id=who, device_id_type=MESH)
-
-    @pl.when(jnp.logical_not(start))
-    def _():
-        to_left.start()
-
-    @pl.when(start)
-    def _():
-        to_relay.start()
-
-    @pl.when(helper)
-    def _():
-        to_relay.wait_recv()
-        onward.start()
-
     for j in range(0, cells, 2 * LANES):
         mix(out[:, j : j + 2 * LANES], (j // LANES, j // LANES + 1), True)
     loads[6].wait()
@@ -310,9 +391,56 @@
             picked = surf[ablk_s[n]].astype(BF16)
             part = jnp.dot(picked, w_v[n], preferred_element_type=F32)
             contrib[pl.ds(n, 8, stride=nb), :] = part
-
-    to_right.wait_recv()
-    to_left.wait_recv()
+        place = toff_v[...] * oblocks + oblk_v[...]
+        onehot = (iota((SPREAD * oblocks, nb), 0) == jnp.broadcast_to(place, (SPREAD * oblocks, nb))).astype(F32)
+        onehot_v[...] = onehot.astype(BF16)
+        for at_side, first in ((start, fields), (end, fields + 2)):
+
+            @pl.when(at_side)
+            def _():
+                for e in range(2):
+                    rows_of = contrib[nb * (first + e) : nb * (first + e + 1), :].astype(BF16)
+                    seam[:, e * LANES : (e + 1) * LANES] = jnp.dot(
+                        onehot.astype(BF16), rows_of, preferred_element_type=F32
+                    )
+
+        @pl.when(end)
+        def _():
+            for d in range(1, REACH + 1):
+                seam_copy(d).start()
+
+    @pl.when(jnp.logical_not(start))
+    def _():
+        to_right.wait_recv()
+        beside[0] = halo[0]
+
+    @pl.when(start)
+    def _():
+        beside[0] = jnp.zeros((8, LANES), F32)
+
+    @pl.when(jnp.logical_not(end))
+    def _():
+        to_left.wait_recv()
+        beside[1] = halo[1]
+
+    @pl.when(end)
+    def _():
+        beside[1] = jnp.zeros((8, LANES), F32)
+
+    def edge_surface(own, before, after):
+        x = jnp.where(place_in < 2, pltpu.roll(before, LANES - 10, 1), own)
+        x = jnp.where(place_in >= 12, pltpu.roll(after, 10, 1), x)
+        near = pltpu.roll(x, 1, 1) + pltpu.roll(x, LANES - 1, 1)
+        far = pltpu.roll(x, 2, 1) + pltpu.roll(x, LANES - 2, 1)
+        z = packed_ops[3] * (packed_ops[0] * x + packed_ops[1] * near + packed_ops[2] * far)
+        for shift in (4, 2, 1):
+            z = z + pltpu.roll(z, shift, 0)
+        z = z + pltpu.roll(z, LANES - GROUP, 1)
+        return jnp.tanh(z).astype(BF16).astype(F32)
+
+    def spread_lane(r, at, height):
+        scale = jnp.broadcast_to(r[:, at : at + 1], (8, LANES))
+        return jnp.concatenate([scale] * (height // 8), axis=0)
 
     def dense_copy(d):
         return pltpu.make_async_remote_copy(
@@ -326,28 +454,17 @@
 
     @pl.when(is_atmos)
     def _():
-        x = jnp.where(place_in < 2, pltpu.roll(halo[0], LANES - 10, 1), pack[...])
-        x = jnp.where(place_in >= 12, pltpu.roll(halo[1], 10, 1), x)
-        near = pltpu.roll(x, 1, 1) + pltpu.roll(x, LANES - 1, 1)
-        far = pltpu.roll(x, 2, 1) + pltpu.roll(x, LANES - 2, 1)
-        z = packed_ops[3] * (packed_ops[0] * x + packed_ops[1] * near + packed_ops[2] * far)
-        for shift in (4, 2, 1):
-            z = z + pltpu.roll(z, shift, 0)
-        z = z + pltpu.roll(z, LANES - GROUP, 1)
-        r = jnp.tanh(z).astype(BF16).astype(F32)
-        place = toff_v[...] * oblocks + oblk_v[...]
-        onehot = (iota((SPREAD * oblocks, nb), 0) == jnp.broadcast_to(place, (SPREAD * oblocks, nb))).astype(F32)
-        onehot = onehot.astype(BF16)
+        r = edge_surface(pack[...], beside[0], beside[1])
+        r = jnp.where(start & (place_in < 4), 0.0, jnp.where(end & (place_in > 9), 0.0, r))
+        placed = onehot_v[...]
         for k in range(fields):
             got = contrib[nb * k : nb * k + nb, :]
             for e, p in enumerate((2, 3, 10, 11)):
                 at = 2 * k * GROUP + p
-                scale = jnp.broadcast_to(r[:, at : at + 1], (8, LANES))
-                scale = jnp.concatenate([scale] * (nb // 8), axis=0)
-                got = got + scale * contrib[nb * (4 + e) : nb * (5 + e), :]
+                got = got + spread_lane(r, at, nb) * contrib[nb * (4 + e) : nb * (5 + e), :]
             hi, lo = split2(got)
-            dense[:, k * LANES : (k + 1) * LANES] = jnp.dot(onehot, hi, preferred_element_type=F32) + jnp.dot(
-                onehot, lo, preferred_element_type=F32
+            dense[:, k * LANES : (k + 1) * LANES] = jnp.dot(placed, hi, preferred_element_type=F32) + jnp.dot(
+                placed, lo, preferred_element_type=F32
             )
         for d in range(1, REACH + 1):
 
@@ -363,14 +480,22 @@
             def _():
                 dense_copy(d).start()
 
+            @pl.when(wanted & (start | end))
+            def _():
+                seam_copy(d).start()
+
+                @pl.when((d < 0) | end)
+                def _():
+                    seam_pack_copy(d).start()
+
         def tell(stage, who, wanted):
             @pl.when(wanted)
             def _():
                 pl.semaphore_signal(known.at[stage], inc=1, device_id=(c, who), device_id_type=MESH)
 
-        upper = spot >= HALF
-        tell(0, right, (spot >= HALF - 1) & (spot < PLANE - 1))
-        tell(1, left, (spot == HALF + 1) | (spot == HALF + 2))
+        upper = jnp.logical_not(lower)
+        tell(0, right, (spot >= HALF - 1) & (spot < PLANE - 1) & (t >= PLANE))
+        tell(1, left, (spot > HALF) & (spot < HALF + 3) & (t >= PLANE))
         for d in (0, -1, 1):
             send(d, inside(d))
         for d in (-2, 2, -3, 3):
@@ -378,7 +503,12 @@
 
         @pl.when(spot < REACH)
         def _():
-            pl.semaphore_wait(known.at[4], REACH - spot)
+            pl.semaphore_wait(known.at[4], jnp.where(start, REACH + 1, REACH - spot))
+
+            @pl.when(start)
+            def _():
+                seam_pack_copy(-REACH - 1).start()
+
             for d in range(1, REACH + 1):
                 send(-d, spot < d)
 
@@ -386,7 +516,7 @@
         def _():
             pl.semaphore_wait(known.at[0], 1)
             tell(2, right, spot < PLANE - 1)
-            dense_copy(-2).start()
+            send(-2, upper)
 
             @pl.when(spot < HALF + 2)
             def _():
@@ -398,12 +528,26 @@
             def _():
                 pl.semaphore_wait(known.at[2], 1)
 
-            dense_copy(-3).start()
+            send(-3, upper)
 
             @pl.when(spot == HALF)
             def _():
                 pl.semaphore_wait(known.at[3], 1)
                 dense_copy(3).start()
+
+    @pl.when(start)
+    def _():
+        to_right.wait_recv()
+
+    @pl.when(helper)
+    def _():
+        to_relay.wait_recv()
+        pl.semaphore_wait(known.at[5], 1)
+        onward.start()
+
+    @pl.when(end)
+    def _():
+        to_left.wait_recv()
 
     hl = halo[0]
     hr = halo[1]
@@ -433,6 +577,20 @@
     def _():
         onward.wait_send()
 
+    @pl.when(is_atmos & (start | end))
+    def _():
+        for d in range(-REACH, REACH + 1):
+            seam_copy(d).wait_send()
+            seam_pack_copy(d).wait_send()
+
+        @pl.when(start)
+        def _():
+            seam_pack_copy(-REACH - 1).wait_send()
+
+        @pl.when(end)
+        def _():
+            seam_pack_copy(REACH + 1).wait_send()
+
     @pl.when(is_atmos)
     def _():
         for d in range(-REACH, REACH + 1):
@@ -440,7 +598,51 @@
 
     @pl.when(is_ocean)
     def _():
-        total = None
+        def seam_part(which):
+            for src in range(comps - 1):
+                pltpu.make_async_remote_copy(
+                    src_ref=seam.at[pl.ds(0, oblocks)],
+                    dst_ref=seam_got.at[2 * src + which],
+                    send_sem=seam_send.at[0],
+                    recv_sem=seam_recv.at[2 * src + which],
+                    device_id=(c, t),
+                    device_id_type=MESH,
+                ).wait_recv()
+            for k in range(fields):
+                cols = slice(k * LANES, (k + 1) * LANES)
+                got = rx[:, cols]
+                for src in range(comps - 1):
+                    r = seam_r[2 * src + which]
+                    for e in range(2):
+                        at = 2 * k * GROUP + (2, 10)[which] + e
+                        got = got + spread_lane(r, at, oblocks) * seam_got[
+                            2 * src + which, :, e * LANES : (e + 1) * LANES
+                        ]
+                rx[:, cols] = got
+
+        rx[...] = jnp.zeros_like(rx)
+
+        @pl.when(near_seam)
+        def _():
+            for slot in range(2 * (comps - 1)):
+                pltpu.make_async_remote_copy(
+                    src_ref=pack,
+                    dst_ref=seam_pack.at[slot],
+                    send_sem=pack_send.at[0],
+                    recv_sem=pack_recv.at[slot],
+                    device_id=(c, t),
+                    device_id_type=MESH,
+                ).wait_recv()
+            for src in range(comps - 1):
+                first, last = seam_pack[2 * src], seam_pack[2 * src + 1]
+                seam_r[2 * src] = edge_surface(first, last, last)
+                seam_r[2 * src + 1] = edge_surface(last, first, first)
+
+        @pl.when(ocean_start)
+        def _():
+            seam_part(0)
+
+        total = rx[...]
         for slot in sorted(range((comps - 1) * SPREAD), key=lambda slot: slot % SPREAD):
             pltpu.make_async_remote_copy(
                 src_ref=dense.at[pl.ds(0, oblocks)],
@@ -450,9 +652,15 @@
                 device_id=(c, t),
                 device_id_type=MESH,
             ).wait_recv()
-            total = recv[slot] if total is None else total + recv[slot]
+            total = total + recv[slot]
         land = mask_v[...].astype(F32)
-        rx[...] = total * jnp.concatenate([land] * fields, axis=1)
+        rx[...] = total
+
+        @pl.when(ocean_end)
+        def _():
+            seam_part(1)
+
+        rx[...] = rx[...] * jnp.concatenate([land] * fields, axis=1)
         for k in range(fields):
             for o in range(oblocks):
                 cols = slice(o * LANES, (o + 1) * LANES)
@@ -491,17 +699,27 @@
                 pltpu.VMEM((8 * nb, LANES), F32),
                 pltpu.VMEM((SPREAD * oblocks, fields * LANES), F32),
                 pltpu.VMEM(((comps - 1) * SPREAD, oblocks, fields * LANES), F32),
+                pltpu.VMEM((4, 8, LANES), F32),
+                pltpu.VMEM((2, 8, LANES), F32),
+                pltpu.VMEM((SPREAD * oblocks, 2 * LANES), F32),
+                pltpu.VMEM((2 * (comps - 1), oblocks, 2 * LANES), F32),
+                pltpu.VMEM((2 * (comps - 1), 8, LANES), F32),
+                pltpu.VMEM((2 * (comps - 1), 8, LANES), F32),
                 pltpu.VMEM((8, LANES), F32),
-                pltpu.VMEM((4, 8, LANES), F32),
+                pltpu.VMEM((SPREAD * oblocks, nb), BF16),
                 pltpu.VMEM((oblocks, fields * LANES), F32),
                 pltpu.SemaphoreType.DMA((11,)),
                 pltpu.SemaphoreType.DMA((2,)),
                 pltpu.SemaphoreType.DMA((2,)),
+                pltpu.SemaphoreType.DMA((SPREAD,)),
+                pltpu.SemaphoreType.DMA((2 * (comps - 1),)),
+                pltpu.SemaphoreType.DMA((SPREAD + 2,)),
+                pltpu.SemaphoreType.DMA((2 * (comps - 1),)),
                 pltpu.SemaphoreType.DMA((2,)),
                 pltpu.SemaphoreType.DMA((1,)),
                 pltpu.SemaphoreType.DMA((SPREAD,)),
                 pltpu.SemaphoreType.DMA(((comps - 1) * SPREAD,)),
-                pltpu.SemaphoreType.REGULAR((5,)),
+                pltpu.SemaphoreType.REGULAR((6,)),
             ],
             compiler_params=pltpu.CompilerParams(collective_id=0, has_side_effects=True),
             name="step",

time: 22.3 us -> 22.1 us (level)
  the two profiles are of different devices: /device:TPU:25 before, /device:TPU:1 now
where the time goes in v5:
time: 22.1 us; the launch traced here: 22 us
  Pallas kernels  21.2 us (96%)
  local copies, waits for them, and re-layouts  0.8 us (4%)
    pallas_call x1, Pallas kernels, local(): pl.pallas_call(functools.partial(kernel, dims), out_shape=pltpu.VMEM((row...  21.2 us
    unnamed x1, local copies, waits for them, and re-layouts  0.8 us

profile of v5, /device:TPU:1, one launch (start us, length us, event | category | flops | bytes accessed | tf_op | source)
XLA Modules:
  0.0 22.0 jit_solution(18047835935071048792)
XLA Ops:
  0.0 21.2 %step.1 = f32[64,2048]{1,0:T(8,128)S(1)} custom-call(f32[64,2048]{1,0:T(8,128)} %bitcast.8, f32[2,4,16]{2,1,0:T(4,128)} %mixing.1, f32[2,16,16]{2,1,0:T(8,128)} %vertical.1, f32[2,4]{1,0:T(2,128)} %flux.1, s32[16]{0:T(128)} %bitcast.11, s32[1,16]{1,0:T(1,128)} %bitcast.12, s32[1,16]{1,0:T(1,128)} %bitcast.13, bf16[16,128,128]{2,1,0:T(8,128)(2,1)} %bitcast.9, ...), custom_call_target="tpu_custom_call" | custom-call | tf_op jit(solution)/shard_map/step/pallas_call | solution.py:679
  21.2 0.8 %copy.11 = f32[1,1,4,16,2048]{4,3,2,1,0:T(8,128)} copy(f32[1,1,4,16,2048]{4,3,2,1,0:T(8,128)S(1)} %bitcast.7) | data formatting | bytes 1048576

commit v6 on v5

--- a/solution.py
+++ b/solution.py
@@ -71,7 +71,7 @@
     seam_pack,
     seam_r,
     relay,
-    onehot_v,
+    borders,
     rx,
     load_sem,
     halo_send,
@@ -192,6 +192,108 @@
         packed = jnp.where(here & (place_in >= 7), pltpu.roll(b, (GROUP * i + 12) % LANES, 1), packed)
     pack[...] = packed
 
+    pl.semaphore_wait(
+        barrier,
+        jnp.where(end, 3, 2)
+        + jnp.where(
+            is_atmos,
+            jnp.where(lower, 1 + REACH + jnp.minimum(spot, PLANE - 1 - spot), 1)
+            + jnp.maximum(spot - (PLANE - 1 - REACH), 0)
+            + jnp.where(end, 1, 0),
+            (comps - 1) * (jnp.maximum(spot - (PLANE - 1 - REACH), 0) + jnp.where(t == tiles - REACH - 1, 1, 0)),
+        ),
+    )
+
+    def pack_copy(way, who):
+        return pltpu.make_async_remote_copy(
+            src_ref=pack,
+            dst_ref=halo.at[way],
+            send_sem=halo_send.at[way],
+            recv_sem=halo_recv.at[way],
+            device_id=(c, who),
+            device_id_type=MESH,
+        )
+
+    to_right = pack_copy(0, right)
+    to_left = pack_copy(1, left)
+    to_right.start()
+
+    to_relay = pltpu.make_async_remote_copy(
+        src_ref=pack,
+        dst_ref=relay,
+        send_sem=relay_send.at[0],
+        recv_sem=relay_recv.at[0],
+        device_id=(c, PLANE - 1),
+        device_id_type=MESH,
+    )
+    onward = pltpu.make_async_remote_copy(
+        src_ref=relay,
+        dst_ref=halo.at[1],
+        send_sem=relay_send.at[1],
+        recv_sem=halo_recv.at[1],
+        device_id=(c, tiles - 1),
+        device_id_type=MESH,
+    )
+
+    @pl.when(jnp.logical_not(start))
+    def _():
+        to_left.start()
+
+    @pl.when(start)
+    def _():
+        to_relay.start()
+
+    @pl.when(end)
+    def _():
+        pl.semaphore_signal(known.at[5], inc=1, device_id=(c, PLANE - 1), device_id_type=MESH)
+
+    side = jnp.where(end, 1, 0)
+
+    def seam_pack_copy(d):
+        return pltpu.make_async_remote_copy(
+            src_ref=pack,
+            dst_ref=seam_pack.at[2 * c + side],
+            send_sem=pack_send.at[d + REACH + 1],
+            recv_sem=pack_recv.at[2 * c + side],
+            device_id=(ocean_row, lax.rem(t + d + tiles, tiles)),
+            device_id_type=MESH,
+        )
+
+    def seam_copy(d):
+        return pltpu.make_async_remote_copy(
+            src_ref=seam.at[pl.ds((d + REACH) * oblocks, oblocks)],
+            dst_ref=seam_got.at[2 * c + side],
+            send_sem=seam_send.at[d + REACH],
+            recv_sem=seam_recv.at[2 * c + side],
+            device_id=(ocean_row, lax.rem(t + d + tiles, tiles)),
+            device_id_type=MESH,
+        )
+
+    @pl.when(is_atmos & end)
+    def _():
+        for d in range(1, REACH + 2):
+            seam_pack_copy(d).start()
+
+    @pl.when(is_atmos & start)
+    def _():
+        for d in range(0, REACH + 1):
+            seam_pack_copy(d).start()
+
+    @pl.when(is_ocean)
+    def _():
+        for d in range(1, REACH + 1):
+
+            @pl.when(spot + d >= PLANE)
+            def _():
+                for src in range(comps - 1):
+                    who = (src, lax.rem(t + d, tiles))
+                    pl.semaphore_signal(known.at[4], inc=1, device_id=who, device_id_type=MESH)
+
+        @pl.when(t == tiles - REACH - 1)
+        def _():
+            for src in range(comps - 1):
+                pl.semaphore_signal(known.at[4], inc=1, device_id=(src, 0), device_id_type=MESH)
+
     loads[3].wait()
     loads[4].wait()
     loads[5].wait()
@@ -271,108 +373,6 @@
                     low, half * moved, 0.0
                 )
 
-    pl.semaphore_wait(
-        barrier,
-        jnp.where(end, 3, 2)
-        + jnp.where(
-            is_atmos,
-            jnp.where(lower, 1 + REACH + jnp.minimum(spot, PLANE - 1 - spot), 1)
-            + jnp.maximum(spot - (PLANE - 1 - REACH), 0)
-            + jnp.where(end, 1, 0),
-            (comps - 1) * (jnp.maximum(spot - (PLANE - 1 - REACH), 0) + jnp.where(t == tiles - REACH - 1, 1, 0)),
-        ),
-    )
-
-    def pack_copy(way, who):
-        return pltpu.make_async_remote_copy(
-            src_ref=pack,
-            dst_ref=halo.at[way],
-            send_sem=halo_send.at[way],
-            recv_sem=halo_recv.at[way],
-            device_id=(c, who),
-            device_id_type=MESH,
-        )
-
-    to_right = pack_copy(0, right)
-    to_left = pack_copy(1, left)
-    to_right.start()
-
-    to_relay = pltpu.make_async_remote_copy(
-        src_ref=pack,
-        dst_ref=relay,
-        send_sem=relay_send.at[0],
-        recv_sem=relay_recv.at[0],
-        device_id=(c, PLANE - 1),
-        device_id_type=MESH,
-    )
-    onward = pltpu.make_async_remote_copy(
-        src_ref=relay,
-        dst_ref=halo.at[1],
-        send_sem=relay_send.at[1],
-        recv_sem=halo_recv.at[1],
-        device_id=(c, tiles - 1),
-        device_id_type=MESH,
-    )
-
-    @pl.when(jnp.logical_not(start))
-    def _():
-        to_left.start()
-
-    @pl.when(start)
-    def _():
-        to_relay.start()
-
-    @pl.when(end)
-    def _():
-        pl.semaphore_signal(known.at[5], inc=1, device_id=(c, PLANE - 1), device_id_type=MESH)
-
-    side = jnp.where(end, 1, 0)
-
-    def seam_pack_copy(d):
-        return pltpu.make_async_remote_copy(
-            src_ref=pack,
-            dst_ref=seam_pack.at[2 * c + side],
-            send_sem=pack_send.at[d + REACH + 1],
-            recv_sem=pack_recv.at[2 * c + side],
-            device_id=(ocean_row, lax.rem(t + d + tiles, tiles)),
-            device_id_type=MESH,
-        )
-
-    def seam_copy(d):
-        return pltpu.make_async_remote_copy(
-            src_ref=seam.at[pl.ds((d + REACH) * oblocks, oblocks)],
-            dst_ref=seam_got.at[2 * c + side],
-            send_sem=seam_send.at[d + REACH],
-            recv_sem=seam_recv.at[2 * c + side],
-            device_id=(ocean_row, lax.rem(t + d + tiles, tiles)),
-            device_id_type=MESH,
-        )
-
-    @pl.when(is_atmos & end)
-    def _():
-        for d in range(1, REACH + 2):
-            seam_pack_copy(d).start()
-
-    @pl.when(is_atmos & start)
-    def _():
-        for d in range(0, REACH + 1):
-            seam_pack_copy(d).start()
-
-    @pl.when(is_ocean)
-    def _():
-        for d in range(1, REACH + 1):
-
-            @pl.when(spot + d >= PLANE)
-            def _():
-                for src in range(comps - 1):
-                    who = (src, lax.rem(t + d, tiles))
-                    pl.semaphore_signal(known.at[4], inc=1, device_id=who, device_id_type=MESH)
-
-        @pl.when(t == tiles - REACH - 1)
-        def _():
-            for src in range(comps - 1):
-                pl.semaphore_signal(known.at[4], inc=1, device_id=(src, 0), device_id_type=MESH)
-
     loads[2].wait()
     for i in range(groups):
         s = slice(8 * i, 8 * i + 8)
@@ -393,16 +393,24 @@
             contrib[pl.ds(n, 8, stride=nb), :] = part
         place = toff_v[...] * oblocks + oblk_v[...]
         onehot = (iota((SPREAD * oblocks, nb), 0) == jnp.broadcast_to(place, (SPREAD * oblocks, nb))).astype(F32)
-        onehot_v[...] = onehot.astype(BF16)
-        for at_side, first in ((start, fields), (end, fields + 2)):
-
-            @pl.when(at_side)
-            def _():
-                for e in range(2):
-                    rows_of = contrib[nb * (first + e) : nb * (first + e + 1), :].astype(BF16)
-                    seam[:, e * LANES : (e + 1) * LANES] = jnp.dot(
-                        onehot.astype(BF16), rows_of, preferred_element_type=F32
-                    )
+        placed = onehot.astype(BF16)
+        hi, lo = split2(contrib[...])
+        for k in range(8):
+            part_k = slice(nb * k, nb * k + nb)
+            got = jnp.dot(placed, hi[part_k], preferred_element_type=F32)
+            if k < fields:
+                got = got + jnp.dot(placed, lo[part_k], preferred_element_type=F32)
+                dense[:, k * LANES : (k + 1) * LANES] = got
+            else:
+                borders[:, (k - fields) * LANES : (k - fields + 1) * LANES] = got
+
+        @pl.when(start)
+        def _():
+            seam[...] = borders[:, 0 : 2 * LANES]
+
+        @pl.when(end)
+        def _():
+            seam[...] = borders[:, 2 * LANES : 4 * LANES]
 
         @pl.when(end)
         def _():
@@ -456,21 +464,27 @@
     def _():
         r = edge_surface(pack[...], beside[0], beside[1])
         r = jnp.where(start & (place_in < 4), 0.0, jnp.where(end & (place_in > 9), 0.0, r))
-        placed = onehot_v[...]
-        for k in range(fields):
-            got = contrib[nb * k : nb * k + nb, :]
-            for e, p in enumerate((2, 3, 10, 11)):
-                at = 2 * k * GROUP + p
-                got = got + spread_lane(r, at, nb) * contrib[nb * (4 + e) : nb * (5 + e), :]
-            hi, lo = split2(got)
-            dense[:, k * LANES : (k + 1) * LANES] = jnp.dot(placed, hi, preferred_element_type=F32) + jnp.dot(
-                placed, lo, preferred_element_type=F32
-            )
+        scales = [[spread_lane(r, 2 * k * GROUP + p, oblocks) for p in (2, 3, 10, 11)] for k in range(fields)]
+
+        def complete(d):
+            part_d = slice((d + REACH) * oblocks, (d + REACH + 1) * oblocks)
+            weights_d = [borders[part_d, e * LANES : (e + 1) * LANES] for e in range(4)]
+            for k in range(fields):
+                got = dense[part_d, k * LANES : (k + 1) * LANES]
+                for e in range(4):
+                    got = got + scales[k][e] * weights_d[e]
+                dense[part_d, k * LANES : (k + 1) * LANES] = got
+
         for d in range(1, REACH + 1):
+            complete(d)
+        for d in range(1, REACH + 1):
 
             @pl.when(spot + d >= PLANE)
             def _():
                 dense_copy(d).start()
+
+        for d in range(-REACH, 1):
+            complete(d)
 
         def inside(d):
             return (spot + d >= 0) & (spot + d < PLANE)
@@ -501,7 +515,7 @@
         for d in (-2, 2, -3, 3):
             send(d, inside(d) & jnp.logical_not(upper))
 
-        @pl.when(spot < REACH)
+        @pl.when((spot < REACH) & jnp.logical_not(start & (c == 0)))
         def _():
             pl.semaphore_wait(known.at[4], jnp.where(start, REACH + 1, REACH - spot))
 
@@ -562,6 +576,15 @@
         rights.append(stencil(f[s, cells - LANES : cells + 2 * LANES], i)[:, LANES : 2 * LANES])
     edge = jnp.concatenate([jnp.concatenate(lefts, axis=0), jnp.concatenate(rights, axis=0)], axis=1)
     mix(edge, (0, ntile - 1), False)
+
+    @pl.when(start & (c == 0))
+    def _():
+        pl.semaphore_wait(known.at[4], REACH + 1)
+        seam_pack_copy(-REACH - 1).start()
+        for d in range(-1, -REACH - 1, -1):
+            dense_copy(d).start()
+            seam_copy(d).start()
+            seam_pack_copy(d).start()
 
     to_right.wait_send()
 
@@ -706,7 +729,7 @@
                 pltpu.VMEM((2 * (comps - 1), 8, LANES), F32),
                 pltpu.VMEM((2 * (comps - 1), 8, LANES), F32),
                 pltpu.VMEM((8, LANES), F32),
-                pltpu.VMEM((SPREAD * oblocks, nb), BF16),
+                pltpu.VMEM((SPREAD * oblocks, 4 * LANES), F32),
                 pltpu.VMEM((oblocks, fields * LANES), F32),
                 pltpu.SemaphoreType.DMA((11,)),
                 pltpu.SemaphoreType.DMA((2,)),

time: 22.1 us -> 21.5 us (0.973)
  the two profiles are of different devices: /device:TPU:1 before, /device:TPU:17 now
where the time goes in v6:
time: 21.5 us; the launch traced here: 21.3 us
  Pallas kernels  20.5 us (95%)
  local copies, waits for them, and re-layouts  0.8 us (4%)
    pallas_call x1, Pallas kernels, local(): pl.pallas_call(functools.partial(kernel, dims), out_shape=pltpu.VMEM((row...  20.5 us
    unnamed x1, local copies, waits for them, and re-layouts  0.8 us

profile of v6, /device:TPU:17, one launch (start us, length us, event | category | flops | bytes accessed | tf_op | source)
XLA Modules:
  0.0 21.3 jit_solution(15634211822549513993)
XLA Ops:
  0.0 20.5 %step.1 = f32[64,2048]{1,0:T(8,128)S(1)} custom-call(f32[64,2048]{1,0:T(8,128)} %bitcast.8, f32[2,4,16]{2,1,0:T(4,128)} %mixing.1, f32[2,16,16]{2,1,0:T(8,128)} %vertical.1, f32[2,4]{1,0:T(2,128)} %flux.1, s32[16]{0:T(128)} %bitcast.11, s32[1,16]{1,0:T(1,128)} %bitcast.12, s32[1,16]{1,0:T(1,128)} %bitcast.13, bf16[16,128,128]{2,1,0:T(8,128)(2,1)} %bitcast.9, ...), custom_call_target="tpu_custom_call" | custom-call | tf_op jit(solution)/shard_map/step/pallas_call | solution.py:702
  20.5 0.8 %copy.11 = f32[1,1,4,16,2048]{4,3,2,1,0:T(8,128)} copy(f32[1,1,4,16,2048]{4,3,2,1,0:T(8,128)S(1)} %bitcast.7) | data formatting | bytes 1048576

commit v7 on v6

--- a/solution.py
+++ b/solution.py
@@ -72,6 +72,7 @@
     seam_r,
     relay,
     borders,
+    base,
     rx,
     load_sem,
     halo_send,
@@ -477,7 +478,6 @@
 
         for d in range(1, REACH + 1):
             complete(d)
-        for d in range(1, REACH + 1):
 
             @pl.when(spot + d >= PLANE)
             def _():
@@ -665,6 +665,15 @@
         def _():
             seam_part(0)
 
+        @pl.when(ocean_end)
+        def _():
+            seam_part(1)
+
+        for k in range(fields):
+            for o in range(oblocks):
+                base[o : o + 1, k * LANES : (k + 1) * LANES] = out[
+                    k * lev : k * lev + 1, o * LANES : (o + 1) * LANES
+                ]
         total = rx[...]
         for slot in sorted(range((comps - 1) * SPREAD), key=lambda slot: slot % SPREAD):
             pltpu.make_async_remote_copy(
@@ -677,17 +686,11 @@
             ).wait_recv()
             total = total + recv[slot]
         land = mask_v[...].astype(F32)
-        rx[...] = total
-
-        @pl.when(ocean_end)
-        def _():
-            seam_part(1)
-
-        rx[...] = rx[...] * jnp.concatenate([land] * fields, axis=1)
+        rx[...] = base[...] + total * jnp.concatenate([land] * fields, axis=1)
         for k in range(fields):
             for o in range(oblocks):
                 cols = slice(o * LANES, (o + 1) * LANES)
-                out[k * lev : k * lev + 1, cols] += rx[o : o + 1, k * LANES : (k + 1) * LANES]
+                out[k * lev : k * lev + 1, cols] = rx[o : o + 1, k * LANES : (k + 1) * LANES]
 
 
 def solution(mesh):
@@ -731,6 +734,7 @@
                 pltpu.VMEM((8, LANES), F32),
                 pltpu.VMEM((SPREAD * oblocks, 4 * LANES), F32),
                 pltpu.VMEM((oblocks, fields * LANES), F32),
+                pltpu.VMEM((oblocks, fields * LANES), F32),
                 pltpu.SemaphoreType.DMA((11,)),
                 pltpu.SemaphoreType.DMA((2,)),
                 pltpu.SemaphoreType.DMA((2,)),

time: 21.5 us -> 21.3 us (level)
  no operation moved by 1% of the time
where the time goes in v7:
time: 21.3 us; the launch traced here: 21.2 us
  Pallas kernels  20.4 us (96%)
  local copies, waits for them, and re-layouts  0.8 us (4%)
    pallas_call x1, Pallas kernels, local(): pl.pallas_call(functools.partial(kernel, dims), out_shape=pltpu.VMEM((row...  20.4 us
    unnamed x1, local copies, waits for them, and re-layouts  0.8 us

profile of v7, /device:TPU:17, one launch (start us, length us, event | category | flops | bytes accessed | tf_op | source)
XLA Modules:
  0.0 21.2 jit_solution(6860368784415965186)
XLA Ops:
  0.0 20.4 %step.1 = f32[64,2048]{1,0:T(8,128)S(1)} custom-call(f32[64,2048]{1,0:T(8,128)} %bitcast.8, f32[2,4,16]{2,1,0:T(4,128)} %mixing.1, f32[2,16,16]{2,1,0:T(8,128)} %vertical.1, f32[2,4]{1,0:T(2,128)} %flux.1, s32[16]{0:T(128)} %bitcast.11, s32[1,16]{1,0:T(1,128)} %bitcast.12, s32[1,16]{1,0:T(1,128)} %bitcast.13, bf16[16,128,128]{2,1,0:T(8,128)(2,1)} %bitcast.9, ...), custom_call_target="tpu_custom_call" | custom-call | tf_op jit(solution)/shard_map/step/pallas_call | solution.py:705
  20.4 0.8 %copy.11 = f32[1,1,4,16,2048]{4,3,2,1,0:T(8,128)} copy(f32[1,1,4,16,2048]{4,3,2,1,0:T(8,128)S(1)} %bitcast.7) | data formatting | bytes 1048576
